TPU v7x, 32 devices: a whole 2x2x4 slice. The times are simulated.
32 devices in a mesh: dp: 8 (over z, y), mp: 4 (over x, core).
Axes of the slice: x: 2, y: 2, z: 4, core: 2. Of those that a mesh axis runs over, the one named last changes fastest.
Arguments:
- sentence_entry_words: bfloat16 [16384, 768], P(('dp', 'mp')), may hold values from -6 to 6
- sentence_present_marks: int32 [1024], P(('dp', 'mp')), may hold values 0 or 1
- picture_present_marks: int32 [1024], P(('dp', 'mp')), may hold values 0 or 1
- matched_picture_positions: int32 [1024], replicated, may hold values from 0 to 1023, each once
- stored_picture_patches: bfloat16 [51200, 768], P(('dp', 'mp')), may hold values from -6 to 6
- log_logit_multiplier: float32 [1], replicated, may hold values from 3.6 to 4.3
- leading_standardizer_stretch: float32 [768], replicated, may hold values from 0.5 to 1.5
- leading_standardizer_shift: float32 [768], replicated, may hold values from -1 to 1
- lookup_coefficients: bfloat16 [768, 768], P(None, 'mp'), may hold values from -0.21875 to 0.21875
- lookup_offset: float32 [768], P('mp'), may hold values from -1 to 1
- address_coefficients: bfloat16 [768, 768], P(None, 'mp'), may hold values from -0.21875 to 0.21875
- content_coefficients: bfloat16 [768, 768], P(None, 'mp'), may hold values from -0.21875 to 0.21875
- content_offset: float32 [768], P('mp'), may hold values from -1 to 1
- mixer_exit_coefficients: bfloat16 [768, 768], P('mp'), may hold values from -0.625 to 0.625
- mixer_exit_offset: float32 [768], replicated, may hold values from -1 to 1
- trailing_standardizer_stretch: float32 [768], replicated, may hold values from 0.5 to 1.5
- trailing_standardizer_shift: float32 [768], replicated, may hold values from -1 to 1
- perceptron_entry_coefficients: bfloat16 [768, 3072], P(None, 'mp'), may hold values from -0.21875 to 0.21875
- perceptron_inner_offset: float32 [3072], P('mp'), may hold values from -1 to 1
- perceptron_exit_coefficients: bfloat16 [3072, 768], P('mp'), may hold values from -0.109375 to 0.109375
- perceptron_exit_offset: float32 [768], replicated, may hold values from -1 to 1
- picture_lookup_coefficients: bfloat16 [768, 768], replicated, may hold values from -0.21875 to 0.21875
- picture_address_coefficients: bfloat16 [768, 768], replicated, may hold values from -0.21875 to 0.21875
- picture_content_coefficients: bfloat16 [768, 768], replicated, may hold values from -0.21875 to 0.21875
- picture_mixer_exit: bfloat16 [768, 768], replicated, may hold values from -0.625 to 0.625
- picture_perceptron_entry: bfloat16 [768, 3072], replicated, may hold values from -0.21875 to 0.21875
- picture_perceptron_exit: bfloat16 [3072, 768], replicated, may hold values from -0.109375 to 0.109375
Outputs:
- loss: float32 [1], replicated
- text_out: bfloat16 [16384, 768], P(('dp', 'mp'))
- text_in_grad: float32 [16384, 768], P(('dp', 'mp'))
- temperature_grad: float32 [1], replicated
- ln1_gain_grad: float32 [768], replicated
- ln1_bias_grad: float32 [768], replicated
- w_query_grad: float32 [768, 768], P(None, 'mp')
- query_bias_grad: float32 [768], P('mp')
- w_key_grad: float32 [768, 768], P(None, 'mp')
- w_value_grad: float32 [768, 768], P(None, 'mp')
- value_bias_grad: float32 [768], P('mp')
- w_attn_out_grad: float32 [768, 768], P('mp')
- attn_out_bias_grad: float32 [768], replicated
- ln2_gain_grad: float32 [768], replicated
- ln2_bias_grad: float32 [768], replicated
- w_hidden_grad: float32 [768, 3072], P(None, 'mp')
- hidden_bias_grad: float32 [3072], P('mp')
- w_proj_grad: float32 [3072, 768], P('mp')
- proj_bias_grad: float32 [768], replicated
Inputs may be any that keep to these rules, and one draw needn't show every extreme that they name: `matched_picture_positions`: each index appears exactly once.
All inputs are finite; a program needn't handle non-finite values. No bound on the sum of `sentence_present_marks` or of `picture_present_marks` on one device may be relied on, other than what follows from the above.
Results may differ from a plain program's by a relative error of at most 0.012.
Values may be sent and summed in bfloat16 or wider, within the bound.
A program may use at most 192 MiB of HBM per device.

v0:
```python
from functools import partial

import jax
import jax.numpy as jnp
from jax import lax
from jax.sharding import PartitionSpec as P

D = 768
HEADS = 12
HD = 64
LEN = 16
PATCHES = 50


def layer_norm(tensor, norm_gain, norm_shift):
    centred = tensor - jnp.mean(tensor, axis=-1, keepdims=True)
    variance = jnp.mean(centred * centred, axis=-1, keepdims=True)
    return centred * lax.rsqrt(variance + 1e-06) * norm_gain + norm_shift


def normalize(pooled):
    return pooled * lax.rsqrt(jnp.sum(pooled * pooled, axis=-1, keepdims=True) + 1e-06)


def product(left, right):
    return jnp.dot(left, right, preferred_element_type=jnp.float32)


def masked_scores(queries, key_rows, causal):
    scores = jnp.einsum(
        "gqhd,gkhd->ghqk", queries, key_rows, preferred_element_type=jnp.float32
    ) * HD ** (-0.5)
    if causal:
        places = jnp.arange(scores.shape[-1], dtype=jnp.int32)
        scores = jnp.where(places[None, :] <= places[:, None], scores, -1e30)
    return scores


def softmax_rows(scores):
    highest = jnp.max(scores, axis=-1, keepdims=True)
    weights = jnp.exp(scores - highest)
    totals = jnp.sum(weights, axis=-1, keepdims=True)
    return (weights / totals, highest + jnp.log(totals))


def masked_softmax(logits, keep_mask):
    masked = jnp.where(keep_mask[None, :] > 0, logits, -1e30)
    highest = jnp.max(masked, axis=-1, keepdims=True)
    weights = jnp.exp(masked - highest)
    totals = jnp.sum(weights, axis=-1, keepdims=True)
    return (weights / totals, highest[:, 0] + jnp.log(totals[:, 0]))


def attention_back(queries, key_rows, value_rows, log_totals, mixed_grad):
    scores = masked_scores(queries, key_rows, True)
    attn_probs = jnp.exp(scores - log_totals)
    probs_grad = jnp.einsum(
        "gqhd,gkhd->ghqk", mixed_grad, value_rows, preferred_element_type=jnp.float32
    )
    value_grad = jnp.einsum(
        "ghqk,gqhd->gkhd",
        attn_probs.astype(jnp.bfloat16),
        mixed_grad,
        preferred_element_type=jnp.float32,
    )
    inner_sum = jnp.sum(attn_probs * probs_grad, axis=-1, keepdims=True)
    score_grad = (attn_probs * (probs_grad - inner_sum)).astype(jnp.bfloat16)
    query_grad = jnp.einsum(
        "ghqk,gkhd->gqhd", score_grad, key_rows, preferred_element_type=jnp.float32
    ) * HD ** (-0.5)
    key_grad = jnp.einsum(
        "ghqk,gqhd->gkhd", score_grad, queries, preferred_element_type=jnp.float32
    ) * HD ** (-0.5)
    return (query_grad, key_grad, value_grad)


def image_embed(stored_picture_patches, frozen):
    (
        picture_lookup_coefficients,
        picture_address_coefficients,
        picture_content_coefficients,
        picture_mixer_exit,
        picture_perceptron_entry,
        picture_perceptron_exit,
    ) = frozen
    tokens = stored_picture_patches.astype(jnp.float32)
    examples = tokens.shape[0] // PATCHES
    normed = layer_norm(tokens, 1.0, 0.0).astype(jnp.bfloat16)
    grid_shape = (examples, PATCHES, HEADS, HD)
    queries = product(normed, picture_lookup_coefficients).astype(jnp.bfloat16).reshape(grid_shape)
    key_rows = (
        product(normed, picture_address_coefficients).astype(jnp.bfloat16).reshape(grid_shape)
    )
    value_rows = (
        product(normed, picture_content_coefficients).astype(jnp.bfloat16).reshape(grid_shape)
    )
    attn_probs, unused_totals = softmax_rows(masked_scores(queries, key_rows, False))
    mixed_heads = jnp.einsum(
        "ghqk,gkhd->gqhd",
        attn_probs.astype(jnp.bfloat16),
        value_rows,
        preferred_element_type=jnp.float32,
    )
    mixed_heads = mixed_heads.reshape(examples * PATCHES, D).astype(jnp.bfloat16)
    middle = tokens + product(mixed_heads, picture_mixer_exit)
    normed_two = layer_norm(middle, 1.0, 0.0).astype(jnp.bfloat16)
    hidden_act = jax.nn.gelu(
        product(normed_two, picture_perceptron_entry), approximate=True
    ).astype(jnp.bfloat16)
    output = middle + product(hidden_act, picture_perceptron_exit)
    return normalize(jnp.mean(output.reshape(examples, PATCHES, D), axis=1)).astype(jnp.bfloat16)


def embed(block_out):
    return normalize(jnp.mean(block_out.reshape(-1, LEN, D), axis=1))


def body(
    sentence_entry_words,
    sentence_present_marks,
    picture_present_marks,
    matched_picture_positions,
    stored_picture_patches,
    log_logit_multiplier,
    leading_standardizer_stretch,
    leading_standardizer_shift,
    lookup_coefficients,
    lookup_offset,
    address_coefficients,
    content_coefficients,
    content_offset,
    mixer_exit_coefficients,
    mixer_exit_offset,
    trailing_standardizer_stretch,
    trailing_standardizer_shift,
    perceptron_entry_coefficients,
    perceptron_inner_offset,
    perceptron_exit_coefficients,
    perceptron_exit_offset,
    picture_lookup_coefficients,
    picture_address_coefficients,
    picture_content_coefficients,
    picture_mixer_exit,
    picture_perceptron_entry,
    picture_perceptron_exit,
):
    local_rows = sentence_entry_words.shape[0]
    own_count = sentence_present_marks.shape[0]
    local_heads = lookup_coefficients.shape[1] // HD
    tokens = sentence_entry_words.astype(jnp.float32)
    normed_one, norm_one_back = jax.vjp(
        layer_norm, tokens, leading_standardizer_stretch, leading_standardizer_shift
    )
    gathered = lax.all_gather(normed_one.astype(jnp.bfloat16), "mp", axis=0, tiled=True)
    all_rows = gathered.shape[0]
    grid_shape = (all_rows // LEN, LEN, local_heads, HD)
    queries = (
        (product(gathered, lookup_coefficients) + lookup_offset)
        .astype(jnp.bfloat16)
        .reshape(grid_shape)
    )
    key_rows = product(gathered, address_coefficients).astype(jnp.bfloat16).reshape(grid_shape)
    value_rows = (
        (product(gathered, content_coefficients) + content_offset)
        .astype(jnp.bfloat16)
        .reshape(grid_shape)
    )
    attn_probs, log_totals = softmax_rows(masked_scores(queries, key_rows, True))
    mixed_heads = jnp.einsum(
        "ghqk,gkhd->gqhd",
        attn_probs.astype(jnp.bfloat16),
        value_rows,
        preferred_element_type=jnp.float32,
    )
    mixed_heads = mixed_heads.reshape(all_rows, local_heads * HD).astype(jnp.bfloat16)
    middle = (
        tokens
        + lax.psum_scatter(
            product(mixed_heads, mixer_exit_coefficients), "mp", scatter_dimension=0, tiled=True
        )
        + mixer_exit_offset
    )
    normed_two, norm_two_back = jax.vjp(
        layer_norm, middle, trailing_standardizer_stretch, trailing_standardizer_shift
    )
    gathered_two = lax.all_gather(normed_two.astype(jnp.bfloat16), "mp", axis=0, tiled=True)
    hidden_pre = product(gathered_two, perceptron_entry_coefficients) + perceptron_inner_offset
    hidden_act, gelu_back = jax.vjp(partial(jax.nn.gelu, approximate=True), hidden_pre)
    hidden_act = hidden_act.astype(jnp.bfloat16)
    output = (
        middle
        + lax.psum_scatter(
            product(
                lax.slice_in_dim(hidden_act, 0, local_rows * lax.axis_size("mp"), axis=0),
                perceptron_exit_coefficients,
            ),
            "mp",
            scatter_dimension=0,
            tiled=True,
        )
        + perceptron_exit_offset
    )
    text_emb, embed_back = jax.vjp(embed, output)
    text_half = text_emb.astype(jnp.bfloat16)
    image_half = image_embed(
        stored_picture_patches,
        (
            picture_lookup_coefficients,
            picture_address_coefficients,
            picture_content_coefficients,
            picture_mixer_exit,
            picture_perceptron_entry,
            picture_perceptron_exit,
        ),
    )
    all_text, all_image, all_tmask, all_imask = (
        lax.all_gather(text_half, ("dp", "mp"), axis=0, tiled=True),
        lax.all_gather(image_half, ("dp", "mp"), axis=0, tiled=True),
        lax.all_gather(
            sentence_present_marks.astype(jnp.bfloat16), ("dp", "mp"), axis=0, tiled=True
        ),
        lax.all_gather(
            picture_present_marks.astype(jnp.bfloat16), ("dp", "mp"), axis=0, tiled=True
        ),
    )
    text_mask = all_tmask.astype(jnp.float32)
    image_mask = all_imask.astype(jnp.float32)
    everyone = text_mask.shape[0]
    order = jnp.arange(everyone, dtype=jnp.int32)
    inverse = jnp.zeros((everyone,), jnp.int32).at[matched_picture_positions].set(order)
    pair_valid = text_mask * image_mask[matched_picture_positions]
    offset = lax.axis_index(("dp", "mp")) * own_count
    own_pair = lax.dynamic_slice_in_dim(matched_picture_positions, offset, own_count, 0)
    own_inverse = lax.dynamic_slice_in_dim(inverse, offset, own_count, 0)
    text_weight = lax.dynamic_slice_in_dim(pair_valid, offset, own_count, 0)
    image_weight = pair_valid[own_inverse]
    logit_multiplier = jnp.exp(log_logit_multiplier[0])
    row_logits = logit_multiplier * jnp.einsum(
        "id,jd->ij", text_half, all_image, preferred_element_type=jnp.float32
    )
    row_probs, row_lse = masked_softmax(row_logits, image_mask)
    row_hits = (order[None, :] == own_pair[:, None]).astype(jnp.float32)
    row_loss = row_lse - jnp.sum(row_hits * row_logits, axis=1)
    row_grad = 0.5 * text_weight[:, None] * (row_probs - row_hits)
    column_logits = logit_multiplier * jnp.einsum(
        "cd,jd->cj", image_half, all_text, preferred_element_type=jnp.float32
    )
    column_probs, column_lse = masked_softmax(column_logits, text_mask)
    column_hits = (order[None, :] == own_inverse[:, None]).astype(jnp.float32)
    column_loss = column_lse - jnp.sum(column_hits * column_logits, axis=1)
    column_grad = 0.5 * image_weight[:, None] * (column_probs - column_hits)
    total_part = 0.5 * (jnp.sum(text_weight * row_loss) + jnp.sum(image_weight * column_loss))
    temp_part = jnp.sum(row_grad * row_logits) + jnp.sum(column_grad * column_logits)
    text_grad = product((logit_multiplier * row_grad).astype(jnp.bfloat16), all_image)
    column_half = (logit_multiplier * column_grad).astype(jnp.bfloat16)
    text_grad = text_grad + lax.psum_scatter(
        jnp.einsum("ci,cd->id", column_half, image_half, preferred_element_type=jnp.float32),
        ("dp", "mp"),
        scatter_dimension=0,
        tiled=True,
    )
    token_grad = embed_back(text_grad)[0]
    proj_bias_grad = jnp.sum(token_grad, axis=0)
    grad_rows = lax.all_gather(token_grad.astype(jnp.bfloat16), "mp", axis=0, tiled=True)
    w_proj_grad = jnp.einsum("rf,rd->fd", hidden_act, grad_rows, preferred_element_type=jnp.float32)
    active_grad = jnp.einsum(
        "rd,fd->rf", grad_rows, perceptron_exit_coefficients, preferred_element_type=jnp.float32
    )
    hidden_grad = gelu_back(active_grad)[0].astype(jnp.bfloat16)
    w_hidden_grad = jnp.einsum(
        "rd,rf->df", gathered_two, hidden_grad, preferred_element_type=jnp.float32
    )
    hidden_bias_grad = jnp.sum(hidden_grad.astype(jnp.float32), axis=0)
    normed_two_grad = lax.psum_scatter(
        jnp.einsum(
            "rf,df->rd",
            hidden_grad,
            perceptron_entry_coefficients,
            preferred_element_type=jnp.float32,
        ),
        "mp",
        scatter_dimension=0,
        tiled=True,
    )
    norm_two_grads = norm_two_back(normed_two_grad)
    middle_grad = token_grad + norm_two_grads[0]
    attn_bias_grad = jnp.sum(middle_grad, axis=0)
    attn_grad_rows = lax.all_gather(middle_grad.astype(jnp.bfloat16), "mp", axis=0, tiled=True)
    w_attn_out_grad = jnp.einsum(
        "rk,rd->kd", mixed_heads, attn_grad_rows, preferred_element_type=jnp.float32
    )
    mixed_grad = jnp.einsum(
        "rd,kd->rk", attn_grad_rows, mixer_exit_coefficients, preferred_element_type=jnp.float32
    )
    mixed_grad = mixed_grad.astype(jnp.bfloat16).reshape(grid_shape)
    query_grad, key_grad, value_grad = attention_back(
        queries, key_rows, value_rows, log_totals, mixed_grad
    )
    query_grad = query_grad.reshape(all_rows, local_heads * HD).astype(jnp.bfloat16)
    key_grad = key_grad.reshape(all_rows, local_heads * HD).astype(jnp.bfloat16)
    value_grad = value_grad.reshape(all_rows, local_heads * HD).astype(jnp.bfloat16)
    w_query_grad = jnp.einsum("rd,rk->dk", gathered, query_grad, preferred_element_type=jnp.float32)
    w_key_grad = jnp.einsum("rd,rk->dk", gathered, key_grad, preferred_element_type=jnp.float32)
    w_value_grad = jnp.einsum("rd,rk->dk", gathered, value_grad, preferred_element_type=jnp.float32)
    query_bias_grad = jnp.sum(query_grad.astype(jnp.float32), axis=0)
    value_bias_grad = jnp.sum(value_grad.astype(jnp.float32), axis=0)
    summed_terms = jnp.einsum(
        "rk,dk->rd", query_grad, lookup_coefficients, preferred_element_type=jnp.float32
    )
    summed_terms = summed_terms + jnp.einsum(
        "rk,dk->rd", key_grad, address_coefficients, preferred_element_type=jnp.float32
    )
    normed_one_grad = lax.psum_scatter(
        summed_terms
        + jnp.einsum(
            "rk,dk->rd", value_grad, content_coefficients, preferred_element_type=jnp.float32
        ),
        "mp",
        scatter_dimension=0,
        tiled=True,
    )
    norm_one_grads = norm_one_back(normed_one_grad)
    text_in_grad = middle_grad + norm_one_grads[0]
    summed = lax.psum(
        (
            w_query_grad,
            w_key_grad,
            w_value_grad,
            query_bias_grad,
            value_bias_grad,
            w_attn_out_grad,
            w_hidden_grad,
            hidden_bias_grad,
            w_proj_grad,
        ),
        "dp",
    )
    shared = lax.psum(
        (
            total_part,
            temp_part,
            norm_one_grads[1],
            norm_one_grads[2],
            attn_bias_grad,
            norm_two_grads[1],
            norm_two_grads[2],
            proj_bias_grad,
        ),
        ("dp", "mp"),
    )
    loss = jnp.reshape(shared[0] / jnp.sum(pair_valid), (1,))
    return (
        loss,
        output.astype(jnp.bfloat16),
        text_in_grad,
        jnp.reshape(shared[1], (1,)),
        shared[2],
        shared[3],
        summed[0],
        summed[3],
        summed[1],
        summed[2],
        summed[4],
        summed[5],
        shared[4],
        shared[5],
        shared[6],
        summed[6],
        summed[7],
        summed[8],
        shared[7],
    )


def solution(mesh):
    in_specs = (
        P(("dp", "mp"), None),
        P(("dp", "mp")),
        P(("dp", "mp")),
        P(),
        P(("dp", "mp"), None),
        P(),
        P(),
        P(),
        P(None, "mp"),
        P("mp"),
        P(None, "mp"),
        P(None, "mp"),
        P("mp"),
        P("mp", None),
        P(),
        P(),
        P(),
        P(None, "mp"),
        P("mp"),
        P("mp", None),
        P(),
        P(),
        P(),
        P(),
        P(),
        P(),
        P(),
    )
    out_specs = (
        P(),
        P(("dp", "mp"), None),
        P(("dp", "mp"), None),
        P(),
        P(),
        P(),
        P(None, "mp"),
        P("mp"),
        P(None, "mp"),
        P(None, "mp"),
        P("mp"),
        P("mp", None),
        P(),
        P(),
        P(),
        P(None, "mp"),
        P("mp"),
        P("mp", None),
        P(),
    )
    return jax.shard_map(body, mesh=mesh, in_specs=in_specs, out_specs=out_specs, check_vma=False)
```

profile of v0, /device:TPU:0, one launch (start us, length us, event | category | flops | bytes accessed | tf_op | source)
XLA Modules:
  0.0 1059.8 jit_solution(18426832418236425114)
XLA Ops:
  13.9 31.3 %all-gather.7.cloned.1.call-done = bf16[2048,768]{1,0:T(8,128)(2,1)} async-done(((bf16[512,768]{1,0:T(8,128)(2,1)}), bf16[2048,768]{1,0:T(8,128)(2,1)}) %all-gather.7.cloned.1.call-update) | async-done | bytes 3145744 | tf_op jit(solution)/shard_map/all_gather | solution.py:154
  55.2 3.9 reshape.229
  59.1 5.0 fusion.71
  77.5 3.9 reshape.228
  87.0 4.9 convert_element_type.173
  91.9 4.9 fusion.124
  96.9 58.9 %reduce-scatter.6.cloned.1.call-done = f32[512,768]{1,0:T(8,128)} async-done(((f32[2048,768]{1,0:T(8,128)}), f32[512,768]{1,0:T(8,128)}) %reduce-scatter.6.cloned.1.call-update) | async-done | bytes 1572880 | tf_op jit(solution)/shard_map/reduce_scatter | solution.py:178
  159.7 28.4 %all-gather.9.cloned.1.call-done = bf16[2048,768]{1,0:T(8,128)(2,1)} async-done(((bf16[512,768]{1,0:T(8,128)(2,1)}), bf16[2048,768]{1,0:T(8,128)(2,1)}) %all-gather.9.cloned.1.call-update) | async-done | bytes 3145744 | tf_op jit(solution)/shard_map/all_gather | solution.py:186
  188.1 8.4 multiply_convert_fusion
  198.1 4.5 fusion.125
  205.9 3.7 convolution_convert_fusion
  209.6 8.7 reshape.273
  218.2 5.7 convolution_convert_fusion.1
  223.9 8.5 reshape.272
  232.5 5.6 convolution_convert_fusion.2
  238.1 16.8 %reshape.271 = bf16[32,50,12,64]{3,2,1,0:T(8,128)(2,1)} reshape(bf16[1600,768]{1,0:T(8,128)(2,1)} %convolution_convert_fusion.2) | data formatting | bytes 4915200 | tf_op jit(solution)/shard_map/reshape | solution.py:95
  254.9 12.3 %fusion.27 = f32[32,12,50,50]{2,3,1,0:T(8,128)} fusion(bf16[32,50,12,64]{3,2,1,0:T(8,128)(2,1)} %reshape.273, bf16[32,50,12,64]{3,2,1,0:T(8,128)(2,1)} %reshape.272), kind=kOutput, calls=%fused_computation.38 | convolution fusion | flops 122880000 | bytes 8755200 | tf_op jit(solution)/shard_map/gqhd,gkhd->ghqk/dot_general | solution.py:30
  267.2 14.7 %fusion.122 = (f32[32,12,50]{2,1,0:T(8,128)S(1)}, f32[32,12,50,50]{2,3,1,0:T(8,128)}) fusion(f32[32,12,50,50]{2,3,1,0:T(8,128)} %fusion.27), kind=kOutput, calls=%fused_computation.210 | output fusion | flops 3840049 | bytes 7756800 | tf_op jit(solution)/shard_map/sub | solution.py:41
  281.9 9.6 convert_bitcast_fusion
  291.5 9.4 copy.128
  300.9 11.6 %convert_element_type.185 = bf16[1600,768]{0,1:T(8,128)(2,1)} reshape(bf16[32,50,12,64]{1,0,3,2:T(8,128)(2,1)} %copy.128) | data formatting | bytes 4915200 | tf_op jit(solution)/shard_map/convert_element_type | solution.py:104
  312.5 5.1 fusion.123
  322.7 23.3 %fusion.35 = f32[1600,768]{1,0:T(8,128)} fusion(f32[1600,768]{1,0:T(8,128)} %copy-done.18, bf16[3072,768]{1,0:T(8,128)(2,1)} %param.53, bf16[768,3072]{1,0:T(8,128)(2,1)} %param.52, f32[1600]{0:T(1024)S(1)} %add_rsqrt_fusion, f32[1600]{0:T(1024)S(1)} %broadcast_multiply_fusion), kind=kOutput, calls=%fused_computation.49 | convolution fusion | flops 15148646400 | bytes 19280384 | tf_op jit(solution)/shard_map/dot_general | solution.py:26
  346.0 5.4 reshape.235
  357.0 39.6 %all-reduce.5 = (bf16[1024]{0:T(1024)(128)(2,1)S(1)}, bf16[1024]{0:T(1024)(128)(2,1)S(1)}) all-reduce(bf16[1024]{0:T(1024)(128)(2,1)S(1)} %dynamic-update-slice.1, bf16[1024]{0:T(1024)(128)(2,1)S(1)} %dynamic-update-slice), channel_id=1, replica_groups=mesh['dp'=8,'mp'=4] {'dp','mp'}, use_global_device_ids=true, to_apply=%add.1 | all-reduce | flops 2048 | bytes 8192
  396.7 4.5 gather_fusion
  401.2 4.3 scatter_custom_fusion
  411.9 22.9 %all-gather.11.cloned.1.call-done = bf16[1024,768]{1,0:T(8,128)(2,1)} async-done(((bf16[32,768]{1,0:T(8,128)(2,1)}), bf16[1024,768]{1,0:T(8,128)(2,1)}) %all-gather.11.cloned.1.call-update) | async-done | bytes 1572880 | tf_op jit(solution)/shard_map/all_gather | solution.py:218
  437.1 104.3 %reduce-scatter.10.cloned.1.call-done = f32[32,768]{1,0:T(8,128)} async-done(((f32[1024,768]{1,0:T(8,128)}), f32[32,768]{1,0:T(8,128)}) %reduce-scatter.10.cloned.1.call-update) | async-done | bytes 98320 | tf_op jit(solution)/shard_map/reduce_scatter | solution.py:256
  544.5 27.6 %all-gather.15.cloned.1.call-done = bf16[2048,768]{1,0:T(8,128)(2,1)} async-done(((bf16[512,768]{1,0:T(8,128)(2,1)}), bf16[2048,768]{1,0:T(8,128)(2,1)}) %all-gather.15.cloned.1.call-update) | async-done | bytes 3145744 | tf_op jit(solution)/shard_map/all_gather | solution.py:264
  572.1 8.8 convert_reduce_fusion.1
  582.6 4.6 fusion.126
  587.2 58.9 %reduce-scatter.12.cloned.1.call-done = f32[512,768]{1,0:T(8,128)} async-done(((f32[2048,768]{1,0:T(8,128)}), f32[512,768]{1,0:T(8,128)}) %reduce-scatter.12.cloned.1.call-update) | async-done | bytes 1572880 | tf_op jit(solution)/shard_map/reduce_scatter | solution.py:274
  654.4 26.7 %all-gather.17.cloned.1.call-done = bf16[2048,768]{1,0:T(8,128)(2,1)} async-done(((bf16[512,768]{1,0:T(8,128)(2,1)}), bf16[2048,768]{1,0:T(8,128)(2,1)}) %all-gather.17.cloned.1.call-update) | async-done | bytes 3145744 | tf_op jit(solution)/shard_map/all_gather | solution.py:288
  681.1 3.9 convolution_convert_fusion.3
  688.5 4.8 fusion.66
  704.5 4.1 convert_element_type.201
  708.7 3.6 fusion.127
  714.8 5.0 convert_element_type.204
  719.8 5.0 fusion.128
  728.3 5.1 convert_element_type.208
  733.4 8.5 add_add_fusion
  742.0 7.1 fusion.133
  749.1 4.2 fusion.134
  765.7 22.4 %all-reduce.3 = (f32[192]{0:T(256)}, f32[192]{0:T(256)}, f32[768]{0:T(1024)}) all-reduce(f32[192]{0:T(256)S(1)} %reduce_sum.414, f32[192]{0:T(256)S(1)} %reduce_sum.416, f32[768]{0:T(1024)S(1)} %get-tuple-element.49), channel_id=1, replica_groups=mesh['dp'=8,'mp'=4] {'dp'}, use_global_device_ids=true, to_apply=%region_47.48 | all-reduce | flops 1152 | bytes 9216 | tf_op jit(solution)/shard_map/psum | solution.py:324
  788.1 12.9 %reduce-scatter.14.cloned.1.call-done = f32[512,768]{1,0:T(8,128)} async-done(((f32[2048,768]{1,0:T(8,128)}), f32[512,768]{1,0:T(8,128)}) %reduce-scatter.14.cloned.1.call-update) | async-done | bytes 1572880 | tf_op jit(solution)/shard_map/reduce_scatter | solution.py:313
  807.2 44.2 %all-reduce.2 = (f32[]{:T(128)}, f32[1]{0:T(128)}, f32[768]{0:T(1024)}, f32[768]{0:T(1024)}, f32[768]{0:T(1024)}, /*index=5*/f32[768]{0:T(1024)}, f32[768]{0:T(1024)}, f32[768]{0:T(1024)}) all-reduce(f32[]{:T(128)S(6)} %mul.407, f32[1]{0:T(128)} %bitcast.9, ...), channel_id=1, replica_groups=mesh['dp'=8,'mp'=4] {'dp','mp'}, use_global_device_ids=true, to_apply=%region_27.28 | all-reduce | flops 4610 | bytes 36880 | tf_op jit(solution)/shard_map/psum | solution.py:338
  852.7 188.0 %all-reduce.8.cloned.1.call-done = (f32[768,192]{0,1:T(8,128)}, f32[768,192]{0,1:T(8,128)}, f32[768,192]{0,1:T(8,128)}, f32[192,768]{1,0:T(8,128)}, f32[768,768]{1,0:T(8,128)}, /*index=5*/f32[768,768]{1,0:T(8,128)}) async-done(((f32[768,192]{0,1:T(8,128)}, f32[768,192]{0,1:T(8,128)}, f32[768,192]{0,1:T(8,128)}, f32[192,768]{1,0:T(8,128)}, f32[768,768]{1,0:T(8,128)}, /*index=5*/f32[768,768]{1,0:T(8,128)}), ...) | async-done | bytes 7077904 | tf_op jit(solution)/shard_map/psum | solution.py:324
  (270 shorter events, 123.0 us)
Async XLA Ops:
  7.2 180.9 %copy-start = (bf16[768,768]{1,0:T(8,128)(2,1)S(1)}, bf16[768,768]{1,0:T(8,128)(2,1)}, u32[]{:S(2)}) copy-start(bf16[768,768]{1,0:T(8,128)(2,1)} %param.44) | copy-start | bytes 3538948
  7.2 38.0 %copy-start.29 = (bf16[768,192]{0,1:T(8,128)(2,1)S(1)}, bf16[768,192]{0,1:T(8,128)(2,1)}, u32[]{:S(2)}) copy-start(bf16[768,192]{0,1:T(8,128)(2,1)} %param.37) | copy-start | bytes 884740
  7.2 38.0 %all-gather.7.cloned.1.call-start = ((), (), s32[]{:S(2)}) async-start(), calls=%async_computation.5 | async-start | bytes 3932160 | tf_op jit(solution)/shard_map/all_gather | solution.py:154
  13.8 142.1 %reduce-scatter.6.cloned.1.call-start = ((), (), s32[]{:S(2)}) async-start(), calls=%async_computation.6 | async-start | bytes 7864320 | tf_op jit(solution)/shard_map/reduce_scatter | solution.py:178
  13.9 55.7 %copy-start.44 = (pred[16,16]{1,0:T(8,128)(4,1)}, pred[16,16]{1,0:T(8,128)(4,1)S(1)}, u32[]{:S(2)}) copy-start(pred[16,16]{1,0:T(8,128)(4,1)S(1)} %iota_compare_fusion.2) | copy-start | bytes 772
  59.1 5.0 copy-start.5
  67.1 6.0 copy-start.31
  67.1 6.0 copy-start.63
  81.4 5.6 copy-start.7
  96.8 59.0 %copy-start.1 = (bf16[512,768]{1,0:T(8,128)(2,1)S(1)}, bf16[512,768]{1,0:T(8,128)(2,1)}, u32[]{:S(2)}) copy-start(bf16[512,768]{1,0:T(8,128)(2,1)} %param.27) | copy-start | bytes 2359300
  96.8 59.0 %copy-start.55 = (f32[768]{0:T(1024)S(1)}, f32[768]{0:T(1024)}, u32[]{:S(2)}) copy-start(f32[768]{0:T(1024)} %param.41) | copy-start | bytes 9220
  96.9 61.3 %copy-start.40 = (f32[768]{0:T(1024)S(1)}, f32[768]{0:T(1024)}, u32[]{:S(2)}) copy-start(f32[768]{0:T(1024)} %param.42) | copy-start | bytes 9220
  96.9 61.3 %copy-start.53 = (f32[768]{0:T(1024)S(1)}, f32[768]{0:T(1024)}, u32[]{:S(2)}) copy-start(f32[768]{0:T(1024)} %param.43) | copy-start | bytes 9220
  96.9 91.2 %all-gather.9.cloned.1.call-start = ((), (), s32[]{:S(2)}) async-start(), calls=%async_computation.7 | async-start | bytes 3932160 | tf_op jit(solution)/shard_map/all_gather | solution.py:186
  157.6 30.5 %copy-start.61 = (f32[768]{0:T(1024)S(1)}, f32[768]{0:T(1024)}, u32[]{:S(2)}) copy-start(f32[768]{0:T(1024)} %param.45) | copy-start | bytes 9220
  157.9 38.5 %copy-start.50 = (f32[512]{0:T(512)}, f32[512]{0:T(512)S(1)}, u32[]{:S(2)}) copy-start(f32[512]{0:T(512)S(1)} %multiply_reduce_fusion.4) | copy-start | bytes 6148
  158.2 38.3 %copy-start.46 = (f32[512]{0:T(512)}, f32[512]{0:T(512)S(1)}, u32[]{:S(2)}) copy-start(f32[512]{0:T(512)S(1)} %fusion.102) | copy-start | bytes 6148
  159.4 160.4 %reduce-scatter.8.cloned.1.call-start = ((), (), s32[]{:S(2)}) async-start(), calls=%async_computation.8 | async-start | bytes 7864320 | tf_op jit(solution)/shard_map/reduce_scatter | solution.py:192
  188.1 10.0 copy-start.60
  202.5 204.4 %all-gather.13.cloned.1.call-start = ((), (), s32[]{:S(2)}) async-start(), calls=%async_computation.10 | async-start | bytes 1622016 | tf_op jit(solution)/shard_map/all_gather | solution.py:217
  267.2 14.7 %copy-start.12 = (bf16[32,50,12,64]{3,2,1,0:T(8,128)(2,1)S(1)}, bf16[32,50,12,64]{3,2,1,0:T(8,128)(2,1)}, u32[]{:S(2)}) copy-start(bf16[32,50,12,64]{3,2,1,0:T(8,128)(2,1)} %reshape.271) | copy-start | bytes 7372804
  322.6 112.2 %all-gather.11.cloned.1.call-start = ((), (), s32[]{:S(2)}) async-start(), calls=%async_computation.9 | async-start | bytes 1622016 | tf_op jit(solution)/shard_map/all_gather | solution.py:218
  351.4 45.3 %copy-start.54 = (s32[1024]{0:T(1024)S(1)}, s32[1024]{0:T(1024)}, u32[]{:S(2)}) copy-start(s32[1024]{0:T(1024)} %param.30) | copy-start | bytes 12292
  355.3 51.6 %copy-start.23 = (bf16[32,768]{1,0:T(8,128)(2,1)S(1)}, bf16[32,768]{1,0:T(8,128)(2,1)}, u32[]{:S(2)}) copy-start(bf16[32,768]{1,0:T(8,128)(2,1)} %multiply_convert_fusion.8) | copy-start | bytes 147460
  355.4 186.1 %reduce-scatter.10.cloned.1.call-start = ((), (), s32[]{:S(2)}) async-start(), calls=%async_computation.11 | async-start | bytes 3244032 | tf_op jit(solution)/shard_map/reduce_scatter | solution.py:256
  409.3 25.5 %copy-start.25 = (bf16[32,768]{1,0:T(8,128)(2,1)S(1)}, bf16[32,768]{1,0:T(8,128)(2,1)}, u32[]{:S(2)}) copy-start(bf16[32,768]{1,0:T(8,128)(2,1)} %multiply_convert_fusion.9) | copy-start | bytes 147460
  411.6 160.5 %all-gather.15.cloned.1.call-start = ((), (), s32[]{:S(2)}) async-start(), calls=%async_computation.12 | async-start | bytes 3932160 | tf_op jit(solution)/shard_map/all_gather | solution.py:264
  544.5 101.7 %reduce-scatter.12.cloned.1.call-start = ((), (), s32[]{:S(2)}) async-start(), calls=%async_computation.13 | async-start | bytes 7864320 | tf_op jit(solution)/shard_map/reduce_scatter | solution.py:274
  587.1 59.0 %copy-start.39 = (f32[512]{0:T(512)S(1)}, f32[512]{0:T(512)}, u32[]{:S(2)}) copy-start(f32[512]{0:T(512)} %copy-done.38) | copy-start | bytes 6148
  587.1 59.0 %copy-start.41 = (f32[768]{0:T(1024)S(1)}, f32[768]{0:T(1024)}, u32[]{:S(2)}) copy-start(f32[768]{0:T(1024)} %param.42) | copy-start | bytes 9220
  587.2 59.0 %copy-start.47 = (f32[512]{0:T(512)S(1)}, f32[512]{0:T(512)}, u32[]{:S(2)}) copy-start(f32[512]{0:T(512)} %copy-done.46) | copy-start | bytes 6148
  587.2 61.2 %copy-start.51 = (f32[512]{0:T(512)S(1)}, f32[512]{0:T(512)}, u32[]{:S(2)}) copy-start(f32[512]{0:T(512)} %copy-done.50) | copy-start | bytes 6148
  587.2 93.9 %all-gather.17.cloned.1.call-start = ((), (), s32[]{:S(2)}) async-start(), calls=%async_computation.14 | async-start | bytes 3932160 | tf_op jit(solution)/shard_map/all_gather | solution.py:288
  651.3 29.8 %copy-start.26 = (bf16[192,768]{1,0:T(8,128)(2,1)S(1)}, bf16[192,768]{1,0:T(8,128)(2,1)}, u32[]{:S(2)}) copy-start(bf16[192,768]{1,0:T(8,128)(2,1)} %param.40) | copy-start | bytes 884740
  652.4 148.6 %reduce-scatter.14.cloned.1.call-start = ((), (), s32[]{:S(2)}) async-start(), calls=%async_computation.15 | async-start | bytes 7864320 | tf_op jit(solution)/shard_map/reduce_scatter | solution.py:313
  719.8 5.0 copy-start.8
  719.8 5.0 copy-start.17
  728.3 5.1 copy-start.32
  742.0 298.7 %all-reduce.8.cloned.1.call-start = ((), (), s32[]{:S(2)}) async-start(), calls=%async_computation.16 | async-start | bytes 14155776 | tf_op jit(solution)/shard_map/psum | solution.py:324
  742.0 7.1 copy-start.57
  742.0 7.1 copy-start.67
  760.7 40.3 %copy-start.2 = (bf16[512,768]{1,0:T(8,128)(2,1)S(1)}, bf16[512,768]{1,0:T(8,128)(2,1)}, u32[]{:S(2)}) copy-start(bf16[512,768]{1,0:T(8,128)(2,1)} %param.27) | copy-start | bytes 2359300
  760.7 40.3 %copy-start.36 = (f32[512]{0:T(512)S(1)}, f32[512]{0:T(512)}, u32[]{:S(2)}) copy-start(f32[512]{0:T(512)} %copy-done.35) | copy-start | bytes 6148
  760.7 40.3 %copy-start.37 = (f32[768]{0:T(1024)S(1)}, f32[768]{0:T(1024)}, u32[]{:S(2)}) copy-start(f32[768]{0:T(1024)} %param.33) | copy-start | bytes 9220
  760.7 42.3 %copy-start.49 = (f32[512]{0:T(512)S(1)}, f32[512]{0:T(512)}, u32[]{:S(2)}) copy-start(f32[512]{0:T(512)} %copy-done.48) | copy-start | bytes 6148
  760.7 42.3 %copy-start.43 = (f32[512]{0:T(512)S(1)}, f32[512]{0:T(512)}, u32[]{:S(2)}) copy-start(f32[512]{0:T(512)} %copy-done.42) | copy-start | bytes 6148
  1040.7 5.9 copy-start.24
  1040.7 6.7 copy-start.21
  (33 other events, 79.4 us)
Sparse Core Ops, SparseCore 0:
  13.9 31.2 all-gather.6
  97.0 58.8 reduce-scatter.5
  159.5 28.4 all-gather.8
  202.7 58.8 reduce-scatter.7
  322.7 54.8 all-gather.12
  380.9 53.8 all-gather.10
  440.2 101.1 reduce-scatter.9
  544.6 27.5 all-gather.14
  587.3 58.8 reduce-scatter.11
  652.5 28.4 all-gather.16
  742.1 58.8 reduce-scatter.13
  807.7 232.9 all-reduce.7
where the time goes:
time: 1070 us; the launch traced here: 1060 us
  waiting for transfers between devices  560 us (52%)
  matrix products  172 us (16%)
  local copies, waits for them, and re-layouts  147 us (14%)
  blocking collectives  106 us (10%)
  other arithmetic  52.9 us (5%)
  between operations  21.2 us (2%)
    psum x1, waiting for transfers between devices, body(): lax.psum((w_query_grad, w_key_grad, w_value_grad, query_bias_grad, value_...  188 us
    reduce_scatter x1, waiting for transfers between devices, body(): lax.psum_scatter(jnp.einsum('ci,cd->id', column_half, image_half, preferr...  104 us
    dot_general x12, matrix products, product(): return jnp.dot(left, right, preferred_element_type=jnp.float32)  72.2 us
    reduce_scatter x1, waiting for transfers between devices, body(): lax.psum_scatter(jnp.einsum('rf,df->rd', hidden_grad, perceptron_entry_co...  58.9 us
    reduce_scatter x1, waiting for transfers between devices, body(): lax.psum_scatter(product(mixed_heads, mixer_exit_coefficients), 'mp', sca...  58.9 us
    psum x1, blocking collectives, body(): lax.psum((total_part, temp_part, norm_one_grads[1], norm_one_grads[2], at...  44.2 us
    unnamed x1, blocking collectives  39.6 us
    all_gather x1, waiting for transfers between devices, body(): lax.all_gather(normed_one.astype(jnp.bfloat16), 'mp', axis=0, tiled=True)  31.3 us
  transfers between devices with their start and end apart: 12, of which 10 were waited for; matrix products, arithmetic and copies ran while one was open for 18% of the time, Pallas kernels for 0%

commit v1 on v0

v1 whole, which is shorter than its diff:
```python
from functools import partial

import jax
import jax.numpy as jnp
from jax import lax
from jax.sharding import PartitionSpec as P

D = 768
HEADS = 12
HD = 64
LEN = 16
PATCHES = 50


def layer_norm(tensor, norm_gain, norm_shift):
    centred = tensor - jnp.mean(tensor, axis=-1, keepdims=True)
    variance = jnp.mean(centred * centred, axis=-1, keepdims=True)
    return centred * lax.rsqrt(variance + 1e-06) * norm_gain + norm_shift


def normalize(pooled):
    return pooled * lax.rsqrt(jnp.sum(pooled * pooled, axis=-1, keepdims=True) + 1e-06)


def product(left, right):
    return jnp.dot(left, right, preferred_element_type=jnp.float32)


def masked_scores(queries, key_rows, causal):
    scores = jnp.einsum(
        "gqhd,gkhd->ghqk", queries, key_rows, preferred_element_type=jnp.float32
    ) * HD ** (-0.5)
    if causal:
        places = jnp.arange(scores.shape[-1], dtype=jnp.int32)
        scores = jnp.where(places[None, :] <= places[:, None], scores, -1e30)
    return scores


def softmax_rows(scores):
    highest = jnp.max(scores, axis=-1, keepdims=True)
    weights = jnp.exp(scores - highest)
    totals = jnp.sum(weights, axis=-1, keepdims=True)
    return (weights / totals, highest + jnp.log(totals))


def attention_back(queries, key_rows, value_rows, log_totals, mixed_grad):
    scores = masked_scores(queries, key_rows, True)
    attn_probs = jnp.exp(scores - log_totals)
    probs_grad = jnp.einsum(
        "gqhd,gkhd->ghqk", mixed_grad, value_rows, preferred_element_type=jnp.float32
    )
    value_grad = jnp.einsum(
        "ghqk,gqhd->gkhd",
        attn_probs.astype(jnp.bfloat16),
        mixed_grad,
        preferred_element_type=jnp.float32,
    )
    inner_sum = jnp.sum(attn_probs * probs_grad, axis=-1, keepdims=True)
    score_grad = (attn_probs * (probs_grad - inner_sum)).astype(jnp.bfloat16)
    query_grad = jnp.einsum(
        "ghqk,gkhd->gqhd", score_grad, key_rows, preferred_element_type=jnp.float32
    ) * HD ** (-0.5)
    key_grad = jnp.einsum(
        "ghqk,gqhd->gkhd", score_grad, queries, preferred_element_type=jnp.float32
    ) * HD ** (-0.5)
    return (query_grad, key_grad, value_grad)


def image_embed(stored_picture_patches, frozen):
    (
        picture_lookup_coefficients,
        picture_address_coefficients,
        picture_content_coefficients,
        picture_mixer_exit,
        picture_perceptron_entry,
        picture_perceptron_exit,
    ) = frozen
    tokens = stored_picture_patches.astype(jnp.float32)
    examples = tokens.shape[0] // PATCHES
    normed = layer_norm(tokens, 1.0, 0.0).astype(jnp.bfloat16)
    grid_shape = (examples, PATCHES, HEADS, HD)
    queries = product(normed, picture_lookup_coefficients).astype(jnp.bfloat16).reshape(grid_shape)
    key_rows = (
        product(normed, picture_address_coefficients).astype(jnp.bfloat16).reshape(grid_shape)
    )
    value_rows = (
        product(normed, picture_content_coefficients).astype(jnp.bfloat16).reshape(grid_shape)
    )
    attn_probs, unused_totals = softmax_rows(masked_scores(queries, key_rows, False))
    mixed_heads = jnp.einsum(
        "ghqk,gkhd->gqhd",
        attn_probs.astype(jnp.bfloat16),
        value_rows,
        preferred_element_type=jnp.float32,
    )
    mixed_heads = mixed_heads.reshape(examples * PATCHES, D).astype(jnp.bfloat16)
    middle = tokens + product(mixed_heads, picture_mixer_exit)
    normed_two = layer_norm(middle, 1.0, 0.0).astype(jnp.bfloat16)
    hidden_act = jax.nn.gelu(
        product(normed_two, picture_perceptron_entry), approximate=True
    ).astype(jnp.bfloat16)
    output = middle + product(hidden_act, picture_perceptron_exit)
    return normalize(jnp.mean(output.reshape(examples, PATCHES, D), axis=1)).astype(jnp.bfloat16)


def embed(block_out):
    return normalize(jnp.mean(block_out.reshape(-1, LEN, D), axis=1))


def body(
    sentence_entry_words,
    sentence_present_marks,
    picture_present_marks,
    matched_picture_positions,
    stored_picture_patches,
    log_logit_multiplier,
    leading_standardizer_stretch,
    leading_standardizer_shift,
    lookup_coefficients,
    lookup_offset,
    address_coefficients,
    content_coefficients,
    content_offset,
    mixer_exit_coefficients,
    mixer_exit_offset,
    trailing_standardizer_stretch,
    trailing_standardizer_shift,
    perceptron_entry_coefficients,
    perceptron_inner_offset,
    perceptron_exit_coefficients,
    perceptron_exit_offset,
    picture_lookup_coefficients,
    picture_address_coefficients,
    picture_content_coefficients,
    picture_mixer_exit,
    picture_perceptron_entry,
    picture_perceptron_exit,
):
    own_count = sentence_present_marks.shape[0]
    mp_count = lax.axis_size("mp")
    rank = lax.axis_index("mp")
    text_mask, image_mask = (
        lax.all_gather(sentence_present_marks.astype(jnp.float32), ("dp", "mp"), axis=0, tiled=True),
        lax.all_gather(picture_present_marks.astype(jnp.float32), ("dp", "mp"), axis=0, tiled=True),
    )
    wide = partial(lax.all_gather, axis_name="mp", axis=1, tiled=True)
    tall = partial(lax.all_gather, axis_name="mp", axis=0, tiled=True)
    w_q, w_k, w_v, w_o = (
        wide(lookup_coefficients),
        wide(address_coefficients),
        wide(content_coefficients),
        tall(mixer_exit_coefficients),
    )
    w_h, w_p = (wide(perceptron_entry_coefficients), tall(perceptron_exit_coefficients))
    b_q, b_v, b_h = (tall(lookup_offset), tall(content_offset), tall(perceptron_inner_offset))
    image_half = image_embed(
        stored_picture_patches,
        (
            picture_lookup_coefficients,
            picture_address_coefficients,
            picture_content_coefficients,
            picture_mixer_exit,
            picture_perceptron_entry,
            picture_perceptron_exit,
        ),
    )
    all_image = lax.all_gather(image_half, ("dp", "mp"), axis=0, tiled=True)
    tokens = sentence_entry_words.astype(jnp.float32)
    all_rows = tokens.shape[0]
    normed_one, norm_one_back = jax.vjp(
        layer_norm, tokens, leading_standardizer_stretch, leading_standardizer_shift
    )
    normed_one = normed_one.astype(jnp.bfloat16)
    grid_shape = (all_rows // LEN, LEN, HEADS, HD)
    queries = (product(normed_one, w_q) + b_q).astype(jnp.bfloat16).reshape(grid_shape)
    key_rows = product(normed_one, w_k).astype(jnp.bfloat16).reshape(grid_shape)
    value_rows = (product(normed_one, w_v) + b_v).astype(jnp.bfloat16).reshape(grid_shape)
    attn_probs, log_totals = softmax_rows(masked_scores(queries, key_rows, True))
    mixed_heads = jnp.einsum(
        "ghqk,gkhd->gqhd",
        attn_probs.astype(jnp.bfloat16),
        value_rows,
        preferred_element_type=jnp.float32,
    )
    mixed_heads = mixed_heads.reshape(all_rows, D).astype(jnp.bfloat16)
    middle = tokens + product(mixed_heads, w_o) + mixer_exit_offset
    normed_two, norm_two_back = jax.vjp(
        layer_norm, middle, trailing_standardizer_stretch, trailing_standardizer_shift
    )
    normed_two = normed_two.astype(jnp.bfloat16)
    hidden_pre = product(normed_two, w_h) + b_h
    hidden_act, gelu_back = jax.vjp(partial(jax.nn.gelu, approximate=True), hidden_pre)
    hidden_act = hidden_act.astype(jnp.bfloat16)
    output = middle + product(hidden_act, w_p) + perceptron_exit_offset
    text_emb, embed_back = jax.vjp(embed, output)
    text_half = text_emb.astype(jnp.bfloat16)

    everyone = text_mask.shape[0]
    order = jnp.arange(everyone, dtype=jnp.int32)
    offset = lax.axis_index(("dp", "mp")) * own_count
    own_pair = lax.dynamic_slice_in_dim(matched_picture_positions, offset, own_count, 0)
    own_text = sentence_present_marks.astype(jnp.float32)
    hits = (order[None, :] == own_pair[:, None]).astype(jnp.float32)
    text_weight = own_text * jnp.sum(hits * image_mask[None, :], axis=1)
    inverse = jnp.zeros((everyone,), jnp.int32).at[matched_picture_positions].set(order)
    image_weight = image_mask * text_mask[inverse]
    logit_multiplier = jnp.exp(log_logit_multiplier[0])
    logits = logit_multiplier * jnp.einsum(
        "id,jd->ij", text_half, all_image, preferred_element_type=jnp.float32
    )
    weights = jnp.exp(logits)
    row_weights = weights * image_mask[None, :]
    row_total = jnp.sum(row_weights, axis=1)
    column_weights = weights * own_text[:, None]
    column_total = lax.psum(jnp.sum(column_weights, axis=0), ("dp", "mp"))
    pair_total = jnp.sum(image_weight)
    safe_row = jnp.where(row_total > 0, row_total, 1.0)
    safe_column = jnp.where(column_total > 0, column_total, 1.0)
    hit_logit = jnp.sum(hits * logits, axis=1)
    column_part = 0.5 * jnp.sum(image_weight * jnp.log(safe_column))
    total_part = 0.5 * jnp.sum(text_weight * jnp.log(safe_row)) - jnp.sum(text_weight * hit_logit)
    row_grad = 0.5 * text_weight[:, None] * (row_weights / safe_row[:, None] - hits)
    column_grad = 0.5 * image_weight[None, :] * (column_weights / safe_column[None, :] - hits)
    temp_part = jnp.sum((row_grad + column_grad) * logits)
    text_grad = product((logit_multiplier * row_grad).astype(jnp.bfloat16), all_image) + product(
        (logit_multiplier * column_grad).astype(jnp.bfloat16), all_image
    )
    token_grad = embed_back(text_grad)[0]
    proj_bias_grad = jnp.sum(token_grad, axis=0)
    grad_rows = token_grad.astype(jnp.bfloat16)
    w_proj_grad = jnp.einsum("rf,rd->fd", hidden_act, grad_rows, preferred_element_type=jnp.float32)
    active_grad = jnp.einsum("rd,fd->rf", grad_rows, w_p, preferred_element_type=jnp.float32)
    hidden_grad = gelu_back(active_grad)[0].astype(jnp.bfloat16)
    w_hidden_grad = jnp.einsum(
        "rd,rf->df", normed_two, hidden_grad, preferred_element_type=jnp.float32
    )
    hidden_bias_grad = jnp.sum(hidden_grad.astype(jnp.float32), axis=0)
    normed_two_grad = jnp.einsum("rf,df->rd", hidden_grad, w_h, preferred_element_type=jnp.float32)
    norm_two_grads = norm_two_back(normed_two_grad)
    middle_grad = token_grad + norm_two_grads[0]
    attn_bias_grad = jnp.sum(middle_grad, axis=0)
    attn_grad_rows = middle_grad.astype(jnp.bfloat16)
    w_attn_out_grad = jnp.einsum(
        "rk,rd->kd", mixed_heads, attn_grad_rows, preferred_element_type=jnp.float32
    )
    mixed_grad = jnp.einsum("rd,kd->rk", attn_grad_rows, w_o, preferred_element_type=jnp.float32)
    mixed_grad = mixed_grad.astype(jnp.bfloat16).reshape(grid_shape)
    query_grad, key_grad, value_grad = attention_back(
        queries, key_rows, value_rows, log_totals, mixed_grad
    )
    query_grad = query_grad.reshape(all_rows, D).astype(jnp.bfloat16)
    key_grad = key_grad.reshape(all_rows, D).astype(jnp.bfloat16)
    value_grad = value_grad.reshape(all_rows, D).astype(jnp.bfloat16)
    back = partial(jnp.einsum, "rd,rk->dk", normed_one, preferred_element_type=jnp.float32)
    w_query_grad, w_key_grad, w_value_grad = (back(query_grad), back(key_grad), back(value_grad))
    query_bias_grad = jnp.sum(query_grad.astype(jnp.float32), axis=0)
    value_bias_grad = jnp.sum(value_grad.astype(jnp.float32), axis=0)
    down = partial(jnp.einsum, "rk,dk->rd", preferred_element_type=jnp.float32)
    normed_one_grad = down(query_grad, w_q) + down(key_grad, w_k) + down(value_grad, w_v)
    norm_one_grads = norm_one_back(normed_one_grad)
    text_in_grad = middle_grad + norm_one_grads[0]

    def share(grad, axis):
        part = lax.psum_scatter(
            grad.astype(jnp.bfloat16), "mp", scatter_dimension=axis, tiled=True
        )
        return lax.psum(part, "dp").astype(jnp.float32)

    shared = lax.psum(
        (
            total_part,
            temp_part,
            norm_one_grads[1],
            norm_one_grads[2],
            attn_bias_grad,
            norm_two_grads[1],
            norm_two_grads[2],
            proj_bias_grad,
            query_bias_grad,
            value_bias_grad,
            hidden_bias_grad,
        ),
        ("dp", "mp"),
    )
    loss = jnp.reshape((shared[0] + column_part) / pair_total, (1,))

    def own(vector):
        return lax.dynamic_slice_in_dim(
            vector, rank * (vector.shape[0] // mp_count), vector.shape[0] // mp_count, 0
        )

    return (
        loss,
        output.astype(jnp.bfloat16),
        text_in_grad,
        jnp.reshape(shared[1], (1,)),
        shared[2],
        shared[3],
        share(w_query_grad, 1),
        own(shared[8]),
        share(w_key_grad, 1),
        share(w_value_grad, 1),
        own(shared[9]),
        share(w_attn_out_grad, 0),
        shared[4],
        shared[5],
        shared[6],
        share(w_hidden_grad, 1),
        own(shared[10]),
        share(w_proj_grad, 0),
        shared[7],
    )


def solution(mesh):
    in_specs = (
        P(("dp", "mp"), None),
        P(("dp", "mp")),
        P(("dp", "mp")),
        P(),
        P(("dp", "mp"), None),
        P(),
        P(),
        P(),
        P(None, "mp"),
        P("mp"),
        P(None, "mp"),
        P(None, "mp"),
        P("mp"),
        P("mp", None),
        P(),
        P(),
        P(),
        P(None, "mp"),
        P("mp"),
        P("mp", None),
        P(),
        P(),
        P(),
        P(),
        P(),
        P(),
        P(),
    )
    out_specs = (
        P(),
        P(("dp", "mp"), None),
        P(("dp", "mp"), None),
        P(),
        P(),
        P(),
        P(None, "mp"),
        P("mp"),
        P(None, "mp"),
        P(None, "mp"),
        P("mp"),
        P("mp", None),
        P(),
        P(),
        P(),
        P(None, "mp"),
        P("mp"),
        P("mp", None),
        P(),
    )
    return jax.shard_map(body, mesh=mesh, in_specs=in_specs, out_specs=out_specs, check_vma=False)
```

time: 1070 us -> 745 us (0.70)
  waiting for transfers between devices: 560 us -> 258 us
  local copies, waits for them, and re-layouts: 147 us -> 110 us
  blocking collectives: 106 us -> 141 us
  matrix products: 172 us -> 160 us
    all_gather x6 -> x7, waiting for transfers between devices: 137 us -> 0.07 us  [the longest x1 0.02 us: body(): tall(mixer_exit_coefficients)]
    psum x1, waiting for transfers between devices: 188 us -> 83.1 us  [share(): return lax.psum(part, 'dp').astype(jnp.float32)]
    reduce_scatter x5 -> x6, waiting for transfers between devices: 235 us -> 171 us  [share(): lax.psum_scatter(grad.astype(jnp.bfloat16), 'mp', scatter_dimension=axis,...]
    convert_element_type x16 -> x9, local copies, waits for them, and re-layouts: 39.3 us -> 20.4 us  [the longest x2 5.97 us: body(): mixed_heads = mixed_heads.reshape(all_rows, D).astype(jnp.bfloat16)]
    psum x1, blocking collectives: 22.4 us -> 39.8 us  [body(): column_total = lax.psum(jnp.sum(column_weights, axis=0), ('dp', 'mp'))]
    dot_general x12 -> x10, matrix products: 51 us -> 37.5 us  [the longest x1 10.2 us: body(): jnp.einsum('rd,fd->rf', grad_rows, w_p, preferred_element_type=jnp.float32)]
    unnamed x1 -> x2, blocking collectives: 39.6 us -> 50.7 us
    dot_general x12 -> x13, matrix products: 72.2 us -> 71.3 us  [product(): return jnp.dot(left, right, preferred_element_type=jnp.float32)]
  transfers between devices with their start and end apart: 12 -> 14, of which waited for: 10 -> 6; matrix products, arithmetic and copies ran while one was open for 18% -> 33% of each run, Pallas kernels for 0% -> 0%
where the time goes in v1:
time: 745 us; the launch traced here: 737 us
  waiting for transfers between devices  258 us (35%)
  matrix products  160 us (21%)
  blocking collectives  141 us (19%)
  local copies, waits for them, and re-layouts  110 us (15%)
  other arithmetic  46 us (6%)
  between operations  21.1 us (3%)
    reduce_scatter x6, waiting for transfers between devices, share(): lax.psum_scatter(grad.astype(jnp.bfloat16), 'mp', scatter_dimension=axis,...  171 us
    psum x1, waiting for transfers between devices, share(): return lax.psum(part, 'dp').astype(jnp.float32)  83.1 us
    dot_general x13, matrix products, product(): return jnp.dot(left, right, preferred_element_type=jnp.float32)  71.3 us
    unnamed x2, blocking collectives  50.7 us
    psum x1, blocking collectives, body(): lax.psum((total_part, temp_part, norm_one_grads[1], norm_one_grads[2], at...  45.1 us
    psum x1, blocking collectives, body(): column_total = lax.psum(jnp.sum(column_weights, axis=0), ('dp', 'mp'))  39.8 us
    convert_element_type x2, local copies, waits for them, and re-layouts, image_embed(): mixed_heads.reshape(examples * PATCHES, D).astype(jnp.bfloat16)  21.4 us
    dot_general x2, matrix products, masked_scores(): jnp.einsum('gqhd,gkhd->ghqk', queries, key_rows, preferred_element_type=j...  15.3 us
  transfers between devices with their start and end apart: 14, of which 6 were waited for; matrix products, arithmetic and copies ran while one was open for 33% of the time, Pallas kernels for 0%

profile of v1, /device:TPU:0, one launch (start us, length us, event | category | flops | bytes accessed | tf_op | source)
XLA Modules:
  0.0 737.5 jit_solution(3353801001150994818)
XLA Ops:
  14.5 3.7 convolution_convert_fusion.2
  18.3 8.5 %reshape.272 = bf16[32,50,12,64]{3,2,1,0:T(8,128)(2,1)} reshape(bf16[1600,768]{1,0:T(8,128)(2,1)} %convolution_convert_fusion.2) | data formatting | bytes 4915200 | tf_op jit(solution)/shard_map/reshape | solution.py:84
  26.8 5.4 convolution_convert_fusion.3
  32.2 8.6 %reshape.271 = bf16[32,50,12,64]{3,2,1,0:T(8,128)(2,1)} reshape(bf16[1600,768]{1,0:T(8,128)(2,1)} %convolution_convert_fusion.3) | data formatting | bytes 4915200 | tf_op jit(solution)/shard_map/reshape | solution.py:82
  40.8 11.8 %fusion.26 = f32[32,12,50,50]{2,3,1,0:T(8,128)} fusion(bf16[32,50,12,64]{3,2,1,0:T(8,128)(2,1)} %reshape.272, bf16[32,50,12,64]{3,2,1,0:T(8,128)(2,1)} %reshape.271), kind=kOutput, calls=%fused_computation.35 | convolution fusion | flops 122880000 | bytes 8755200 | tf_op jit(solution)/shard_map/gqhd,gkhd->ghqk/dot_general | solution.py:30
  52.7 15.2 %fusion.112 = (f32[32,12,50]{2,1,0:T(8,128)S(1)}, f32[32,12,50,50]{2,3,1,0:T(8,128)}) fusion(f32[32,12,50,50]{2,3,1,0:T(8,128)} %fusion.26), kind=kOutput, calls=%fused_computation.197 | output fusion | flops 3840049 | bytes 7756800 | tf_op jit(solution)/shard_map/sub | solution.py:41
  67.9 3.6 convolution_convert_fusion.4
  71.5 8.5 %reshape.270 = bf16[32,50,12,64]{3,2,1,0:T(8,128)(2,1)} reshape(bf16[1600,768]{1,0:T(8,128)(2,1)} %convolution_convert_fusion.4) | data formatting | bytes 4915200 | tf_op jit(solution)/shard_map/reshape | solution.py:87
  80.0 9.3 %convert_bitcast_fusion = bf16[32,50,12,64]{3,1,2,0:T(8,128)(2,1)} fusion(f32[32,12,50,50]{2,3,1,0:T(8,128)} %get-tuple-element.69, f32[32,12,50]{2,1,0:T(8,128)S(1)} %get-tuple-element.68, bf16[32,50,12,64]{3,2,1,0:T(8,128)(2,1)} %reshape.270), kind=kOutput, calls=%fused_computation.39 | convolution fusion | flops 126028800 | bytes 8832000 | tf_op jit(solution)/shard_map/ghqk,gkhd->gqhd/dot_general | solution.py:90
  89.3 9.6 %copy.116 = bf16[32,50,12,64]{1,0,3,2:T(8,128)(2,1)} copy(bf16[32,50,12,64]{3,1,2,0:T(8,128)(2,1)} %convert_bitcast_fusion) | data formatting | bytes 4915200 | tf_op jit(solution)/shard_map/convert_element_type | solution.py:96
  98.9 11.7 %convert_element_type.211 = bf16[1600,768]{0,1:T(8,128)(2,1)} reshape(bf16[32,50,12,64]{1,0,3,2:T(8,128)(2,1)} %copy.116) | data formatting | bytes 4915200 | tf_op jit(solution)/shard_map/convert_element_type | solution.py:96
  110.7 4.8 fusion.113
  117.7 23.4 %fusion.34 = f32[1600,768]{1,0:T(8,128)} fusion(f32[1600,768]{1,0:T(8,128)} %copy-done.14, bf16[3072,768]{1,0:T(8,128)(2,1)} %param.53, bf16[768,3072]{1,0:T(8,128)(2,1)} %param.52, f32[1600]{0:T(1024)S(1)} %add_rsqrt_fusion, f32[1600]{0:T(1024)S(1)} %broadcast_multiply_fusion), kind=kOutput, calls=%fused_computation.48 | convolution fusion | flops 15148646400 | bytes 19280384 | tf_op jit(solution)/shard_map/dot_general | solution.py:26
  141.1 5.4 reshape.231
  146.6 3.2 reduce_sum.395
  151.5 42.6 %all-reduce = f32[1024]{0:T(1024)S(1)} all-reduce(f32[1024]{0:T(1024)S(1)} %convert_dynamic-update-slice_fusion), channel_id=1, replica_groups=mesh['dp'=8,'mp'=4] {'dp','mp'}, use_global_device_ids=true, to_apply=%add | all-reduce | flops 1024 | bytes 8192
  195.9 5.5 all-gather
  202.2 4.3 scatter_custom_fusion
  208.2 8.0 %all-reduce.6 = (f32[768]{0:T(1024)S(1)}, f32[768]{0:T(1024)S(1)}) all-reduce(f32[768]{0:T(1024)S(1)} %dynamic-update-slice.2, f32[768]{0:T(1024)S(1)} %dynamic-update-slice.1), channel_id=1, replica_groups=mesh['dp'=8,'mp'=4] {'mp'}, use_global_device_ids=true, to_apply=%add.2 | all-reduce | flops 1536 | bytes 12288
  229.7 3.5 fusion.114
  237.9 4.1 convert_element_type.199
  242.0 2.7 fusion.115
  246.8 8.2 %fusion.99 = f32[512,3072]{1,0:T(8,128)} fusion(bf16[768,3072]{1,0:T(8,128)(2,1)} %all-gather.17.cloned.1.call-done, f32[512,768]{1,0:T(8,128)} %copy-done.11, f32[768]{0:T(1024)S(1)} %copy-done.85, f32[768]{0:T(1024)S(1)} %copy-done.65, f32[512]{0:T(512)S(1)} %fusion.92, f32[512]{0:T(512)S(1)} %broadcast_multiply_fusion.3), kind=kOutput, calls=%fused_computation.194 | convolution fusion | flops 2417885184 | bytes 12593152 | tf_op jit(solution)/shard_map/dot_general | solution.py:26
  255.1 9.6 %bitcast_reduce_fusion = (f32[32,768]{1,0:T(8,128)S(1)}, bf16[512,768]{1,0:T(8,128)(2,1)}) fusion(f32[768]{0:T(1024)S(1)} %copy-done.82, f32[512,768]{1,0:T(8,128)} %copy-done.11, bf16[3072,768]{1,0:T(8,128)(2,1)} %all-gather.19.cloned.1.call-done, f32[512,3072]{1,0:T(8,128)} %fusion.99, f32[3072]{0:T(1024)S(1)} %bitcast.68), kind=kOutput, calls=%fused_computation.87 | convolution fusion | flops 2433196032 | bytes 13483008 | tf_op jit(solution)/shard_map/dot_general | solution.py:26
  266.0 2.7 multiply_reduce_fusion.7
  271.1 39.8 %all-reduce.5 = (f32[1024]{0:T(1024)}, f32[1024]{0:T(1024)S(1)}) all-reduce(f32[1024]{0:T(1024)} %get-tuple-element.28, f32[1024]{0:T(1024)} %copy-done.47), channel_id=1, replica_groups=mesh['dp'=8,'mp'=4] {'dp','mp'}, use_global_device_ids=true, to_apply=%region_24.25 | all-reduce | flops 2048 | bytes 16384 | tf_op jit(solution)/shard_map/psum | solution.py:215
  310.8 9.0 %gather_fusion = f32[1024]{0:T(1024)} fusion(f32[1024]{0:T(1024)S(1)} %get-tuple-element.47, s32[1024]{0:T(1024)} %fusion.88), kind=kCustom, calls=%fused_computation | custom fusion | bytes 12288 | tf_op jit(solution)/shard_map/gather | solution.py:206
  325.0 10.2 %convert_reduce_fusion.1 = (f32[3072]{0:T(1024)}, bf16[512,3072]{1,0:T(8,128)(2,1)S(1)}) fusion(f32[512,3072]{1,0:T(8,128)} %fusion.99, f32[3072]{0:T(1024)S(1)} %bitcast.69, bf16[512,768]{1,0:T(8,128)(2,1)S(1)} %bitcast_convert_fusion, bf16[3072,768]{1,0:T(8,128)(2,1)} %all-gather.19.cloned.1.call-done), kind=kOutput, calls=%fused_computation.30 | convolution fusion | flops 2452091904 | bytes 14966784 | tf_op jit(solution)/shard_map/rd,fd->rf/dot_general | solution.py:232
  335.2 3.5 multiply_reduce_fusion.3
  343.4 3.9 reshape.234
  347.3 3.7 multiply_reduce_fusion.2
  356.0 3.9 convert_element_type.226
  359.9 3.3 convolution_convert_fusion.10
  363.4 3.0 fusion.60
  368.3 3.9 convert_element_type.229
  372.2 3.4 convolution_convert_fusion.9
  375.7 2.7 convert_reduce_fusion.2
  381.1 3.2 convolution_convert_fusion.8
  384.4 3.1 convolution_convert_fusion.7
  387.6 6.5 convolution_convert_fusion.1
  395.3 8.8 %convolution_convert_fusion = bf16[3072,768]{1,0:T(8,128)(2,1)} fusion(bf16[512,768]{1,0:T(8,128)(2,1)S(1)} %copy-done.29, f32[512,3072]{1,0:T(8,128)} %fusion.99, f32[3072]{0:T(1024)S(1)} %bitcast.70), kind=kOutput, calls=%fused_computation.42 | convolution fusion | flops 2434007040 | bytes 11808768 | tf_op jit(solution)/shard_map/rf,rd->fd/dot_general | solution.py:231
  404.2 13.8 %reduce-scatter.9.cloned.1.call-done = bf16[768,192]{0,1:T(8,128)(2,1)} async-done(((bf16[768,768]{0,1:T(8,128)(2,1)}), bf16[768,192]{0,1:T(8,128)(2,1)}) %reduce-scatter.9.cloned.1.call-update) | async-done | bytes 294928 | tf_op jit(solution)/shard_map/reduce_scatter | solution.py:264
  418.0 28.6 %reduce-scatter.11.cloned.1.call-done = bf16[768,192]{0,1:T(8,128)(2,1)} async-done(((bf16[768,768]{0,1:T(8,128)(2,1)}), bf16[768,192]{0,1:T(8,128)(2,1)}) %reduce-scatter.11.cloned.1.call-update) | async-done | bytes 294928 | tf_op jit(solution)/shard_map/reduce_scatter | solution.py:264
  446.6 28.2 %reduce-scatter.13.cloned.1.call-done = bf16[192,768]{1,0:T(8,128)(2,1)} async-done(((bf16[768,768]{1,0:T(8,128)(2,1)}), bf16[192,768]{1,0:T(8,128)(2,1)}) %reduce-scatter.13.cloned.1.call-update) | async-done | bytes 294928 | tf_op jit(solution)/shard_map/reduce_scatter | solution.py:264
  474.9 50.3 %reduce-scatter.15.cloned.1.call-done = bf16[768,768]{1,0:T(8,128)(2,1)} async-done(((bf16[768,3072]{1,0:T(8,128)(2,1)}), bf16[768,768]{1,0:T(8,128)(2,1)}) %reduce-scatter.15.cloned.1.call-update) | async-done | bytes 1179664 | tf_op jit(solution)/shard_map/reduce_scatter | solution.py:264
  525.1 50.5 %reduce-scatter.17.cloned.1.call-done = bf16[768,768]{1,0:T(8,128)(2,1)} async-done(((bf16[3072,768]{1,0:T(8,128)(2,1)}), bf16[768,768]{1,0:T(8,128)(2,1)}) %reduce-scatter.17.cloned.1.call-update) | async-done | bytes 1179664 | tf_op jit(solution)/shard_map/reduce_scatter | solution.py:264
  587.8 45.1 %all-reduce.4 = (f32[]{:T(128)}, f32[1]{0:T(128)}, f32[768]{0:T(1024)}, f32[768]{0:T(1024)}, f32[768]{0:T(1024)S(1)}, /*index=5*/f32[768]{0:T(1024)S(1)}, f32[76...) all-reduce(f32[]{:T(128)S(6)} %sub.88, ...), channel_id=1, replica_groups=mesh['dp'=8,'mp'=4] {'dp','mp'}, use_global_device_ids=true, to_apply=%region_21.22 | all-reduce | flops 9218 | bytes 73744 | tf_op jit(solution)/shard_map/psum | solution.py:269
  636.9 83.1 %all-reduce.10.cloned.1.call-done = (bf16[768,192]{0,1:T(8,128)(2,1)}, bf16[768,192]{0,1:T(8,128)(2,1)}, bf16[768,192]{0,1:T(8,128)(2,1)}, bf16[192,768]{1,0:T(8...) async-done(((bf16[768,192]{0,1:T(8,128)(2,1)}, bf16[768,192]{0,1:T(8,128)(2,1)}, bf16[768,192]{0,1:T(8,128)(2,1)}, bf16[192,768]{1,0:T(8,128)(2,1)}, ...) | async-done | bytes 3538960 | tf_op jit(solution)/shard_map/psum | solution.py:267
  (305 shorter events, 80.8 us)
Async XLA Ops:
  7.2 103.5 %copy-start = (bf16[768,768]{1,0:T(8,128)(2,1)S(1)}, bf16[768,768]{1,0:T(8,128)(2,1)}, u32[]{:S(2)}) copy-start(bf16[768,768]{1,0:T(8,128)(2,1)} %param.51) | copy-start | bytes 3538948
  7.2 209.1 %all-gather.13.cloned.1.call-start = ((), (), s32[]{:S(2)}) async-start(), calls=%async_computation.8 | async-start | bytes 1474560 | tf_op jit(solution)/shard_map/all_gather | solution.py:150
  7.9 212.8 %all-gather.11.cloned.1.call-start = ((), (), s32[]{:S(2)}) async-start(), calls=%async_computation.7 | async-start | bytes 1474560 | tf_op jit(solution)/shard_map/all_gather | solution.py:149
  8.7 216.5 %all-gather.9.cloned.1.call-start = ((), (), s32[]{:S(2)}) async-start(), calls=%async_computation.6 | async-start | bytes 1474560 | tf_op jit(solution)/shard_map/all_gather | solution.py:151
  9.4 232.6 %all-gather.15.cloned.1.call-start = ((), (), s32[]{:S(2)}) async-start(), calls=%async_computation.9 | async-start | bytes 1474560 | tf_op jit(solution)/shard_map/all_gather | solution.py:152
  10.0 236.8 %all-gather.17.cloned.1.call-start = ((), (), s32[]{:S(2)}) async-start(), calls=%async_computation.10 | async-start | bytes 5898240 | tf_op jit(solution)/shard_map/all_gather | solution.py:154
  10.6 244.4 %all-gather.19.cloned.1.call-start = ((), (), s32[]{:S(2)}) async-start(), calls=%async_computation.11 | async-start | bytes 5898240 | tf_op jit(solution)/shard_map/all_gather | solution.py:154
  11.2 254.8 %all-gather.21.cloned.1.call-start = ((), (), s32[]{:S(2)}) async-start(), calls=%async_computation.12 | async-start | bytes 1622016 | tf_op jit(solution)/shard_map/all_gather | solution.py:167
  18.3 8.6 %copy-start.78 = (bf16[768,768]{1,0:T(8,128)(2,1)S(1)}, bf16[768,768]{1,0:T(8,128)(2,1)}, u32[]{:S(2)}) copy-start(bf16[768,768]{1,0:T(8,128)(2,1)} %param.48) | copy-start | bytes 3538948
  52.7 15.2 %copy-start.8 = (bf16[1600,768]{1,0:T(8,128)(2,1)S(1)}, bf16[1600,768]{1,0:T(8,128)(2,1)}, u32[]{:S(2)}) copy-start(bf16[1600,768]{1,0:T(8,128)(2,1)} %param.31) | copy-start | bytes 7372804
  52.7 15.2 %copy-start.79 = (bf16[768,768]{1,0:T(8,128)(2,1)S(1)}, bf16[768,768]{1,0:T(8,128)(2,1)}, u32[]{:S(2)}) copy-start(bf16[768,768]{1,0:T(8,128)(2,1)} %param.50) | copy-start | bytes 3538948
  146.5 4.9 copy-start.87
  146.5 47.7 %copy-start.64 = (s32[1024]{0:T(1024)S(1)}, s32[1024]{0:T(1024)}, u32[]{:S(2)}) copy-start(s32[1024]{0:T(1024)} %param.30) | copy-start | bytes 12292
  146.5 48.3 %copy-start.2 = (bf16[512,768]{1,0:T(8,128)(2,1)S(1)}, bf16[512,768]{1,0:T(8,128)(2,1)}, u32[]{:S(2)}) copy-start(bf16[512,768]{1,0:T(8,128)(2,1)} %param.27) | copy-start | bytes 2359300
  146.5 48.8 %copy-start.88 = (u32[32]{0:T(128)S(1)}, u32[32]{0:T(128)}, u32[]{:S(2)}) copy-start(u32[32]{0:T(128)} %constant.94) | copy-start | bytes 388
  146.5 49.4 %copy-start.63 = (f32[768]{0:T(1024)S(1)}, f32[768]{0:T(1024)}, u32[]{:S(2)}) copy-start(f32[768]{0:T(1024)} %param.45) | copy-start | bytes 9220
  146.5 61.2 %copy-start.72 = (f32[192]{0:T(256)S(1)}, f32[192]{0:T(256)}, u32[]{:S(2)}) copy-start(f32[192]{0:T(256)} %param.36) | copy-start | bytes 2308
  146.5 61.5 %copy-start.73 = (f32[192]{0:T(256)S(1)}, f32[192]{0:T(256)}, u32[]{:S(2)}) copy-start(f32[192]{0:T(256)} %param.39) | copy-start | bytes 2308
  146.6 69.7 %copy-start.34 = (f32[768]{0:T(1024)S(1)}, f32[768]{0:T(1024)}, u32[]{:S(2)}) copy-start(f32[768]{0:T(1024)} %param.33) | copy-start | bytes 9220
  146.6 69.7 %copy-start.83 = (f32[768]{0:T(1024)S(1)}, f32[768]{0:T(1024)}, u32[]{:S(2)}) copy-start(f32[768]{0:T(1024)} %param.34) | copy-start | bytes 9220
  150.7 253.6 %reduce-scatter.7.cloned.1.call-start = ((), (), s32[]{:S(2)}) async-start(), calls=%async_computation.13 | async-start | bytes 1474560 | tf_op jit(solution)/shard_map/reduce_scatter | solution.py:264
  195.3 21.0 %copy-start.43 = (f32[512]{0:T(512)}, f32[512]{0:T(512)S(1)}, u32[]{:S(2)}) copy-start(f32[512]{0:T(512)S(1)} %fusion.54) | copy-start | bytes 6148
  195.3 29.9 %copy-start.39 = (f32[512]{0:T(512)}, f32[512]{0:T(512)S(1)}, u32[]{:S(2)}) copy-start(f32[512]{0:T(512)S(1)} %fusion.91) | copy-start | bytes 6148
  201.4 53.6 %copy-start.49 = (f32[4,1,768]{2,1,0:T(1,128)}, f32[4,1,768]{2,1,0:T(1,128)S(1)}, u32[]{:S(2)}) copy-start(f32[4,1,768]{2,1,0:T(1,128)S(1)} %all-gather) | copy-start | bytes 36868
  244.7 10.3 %copy-start.41 = (f32[512]{0:T(512)}, f32[512]{0:T(512)S(1)}, u32[]{:S(2)}) copy-start(f32[512]{0:T(512)S(1)} %broadcast_multiply_fusion.3) | copy-start | bytes 6148
  246.7 8.3 %copy-start.52 = (f32[512]{0:T(512)}, f32[512]{0:T(512)S(1)}, u32[]{:S(2)}) copy-start(f32[512]{0:T(512)S(1)} %fusion.92) | copy-start | bytes 6148
  246.8 8.3 %copy-start.82 = (f32[768]{0:T(1024)S(1)}, f32[768]{0:T(1024)}, u32[]{:S(2)}) copy-start(f32[768]{0:T(1024)} %param.47) | copy-start | bytes 9220
  255.1 11.0 %copy-start.55 = (s32[32]{0:T(128)S(1)}, s32[32]{0:T(128)}, u32[]{:S(2)}) copy-start(s32[32]{0:T(128)} %dynamic_slice.12) | copy-start | bytes 388
  268.7 54.5 %copy-start.17 = (f32[32,1024]{1,0:T(8,128)}, f32[32,1024]{1,0:T(8,128)S(1)}, u32[]{:S(2)}) copy-start(f32[32,1024]{1,0:T(8,128)S(1)} %get-tuple-element.78) | copy-start | bytes 393220
  319.8 4.9 copy-start.20
  319.8 4.9 copy-start.74
  324.7 10.4 %slice-start = ((s8[4718592]{0:T(1024)(128)(4,1)}), s8[4194304]{0:T(1024)(128)(4,1)S(1)}, s32[]{:S(2)}) async-start(s8[4718592]{0:T(1024)(128)(4,1)} %bitcast.71), calls=%async_computation.20 | async-start | bytes 8388608
  324.9 10.2 %copy-start.28 = (bf16[512,768]{1,0:T(8,128)(2,1)}, bf16[512,768]{1,0:T(8,128)(2,1)S(1)}, u32[]{:S(2)}) copy-start(bf16[512,768]{1,0:T(8,128)(2,1)S(1)} %bitcast_convert_fusion) | copy-start | bytes 2359300
  324.9 10.2 %copy-start.12 = (f32[512,768]{1,0:T(8,128)S(1)}, f32[512,768]{1,0:T(8,128)}, u32[]{:S(2)}) copy-start(f32[512,768]{1,0:T(8,128)} %copy-done.11) | copy-start | bytes 4718596
  324.9 10.2 %copy-start.42 = (f32[512]{0:T(512)S(1)}, f32[512]{0:T(512)}, u32[]{:S(2)}) copy-start(f32[512]{0:T(512)} %copy-done.41) | copy-start | bytes 6148
  324.9 10.2 %copy-start.53 = (f32[512]{0:T(512)S(1)}, f32[512]{0:T(512)}, u32[]{:S(2)}) copy-start(f32[512]{0:T(512)} %copy-done.52) | copy-start | bytes 6148
  325.0 10.2 %copy-start.66 = (f32[768]{0:T(1024)S(1)}, f32[768]{0:T(1024)}, u32[]{:S(2)}) copy-start(f32[768]{0:T(1024)} %param.42) | copy-start | bytes 9220
  325.0 10.2 %slice-start.1 = ((s8[4718592]{0:T(1024)(128)(4,1)}), s8[524288]{0:T(1024)(128)(4,1)S(1)}, s32[]{:S(2)}) async-start(s8[4718592]{0:T(1024)(128)(4,1)} %bitcast.71), calls=%async_computation.21 | async-start | bytes 1048576
  363.3 54.7 %reduce-scatter.9.cloned.1.call-start = ((), (), s32[]{:S(2)}) async-start(), calls=%async_computation.14 | async-start | bytes 1474560 | tf_op jit(solution)/shard_map/reduce_scatter | solution.py:264
  375.6 71.0 %reduce-scatter.11.cloned.1.call-start = ((), (), s32[]{:S(2)}) async-start(), calls=%async_computation.15 | async-start | bytes 1474560 | tf_op jit(solution)/shard_map/reduce_scatter | solution.py:264
  384.4 90.5 %reduce-scatter.13.cloned.1.call-start = ((), (), s32[]{:S(2)}) async-start(), calls=%async_computation.16 | async-start | bytes 1474560 | tf_op jit(solution)/shard_map/reduce_scatter | solution.py:264
  387.5 137.6 %reduce-scatter.15.cloned.1.call-start = ((), (), s32[]{:S(2)}) async-start(), calls=%async_computation.17 | async-start | bytes 5898240 | tf_op jit(solution)/shard_map/reduce_scatter | solution.py:264
  394.2 181.5 %reduce-scatter.17.cloned.1.call-start = ((), (), s32[]{:S(2)}) async-start(), calls=%async_computation.18 | async-start | bytes 5898240 | tf_op jit(solution)/shard_map/reduce_scatter | solution.py:264
  404.1 171.6 %copy-start.54 = (f32[12,64]{1,0:T(8,128)S(1)}, f32[12,64]{1,0:T(8,128)}, u32[]{:S(2)}) copy-start(f32[12,64]{1,0:T(8,128)} %get-tuple-element.85) | copy-start | bytes 9220
  404.1 171.7 %copy-start.31 = (bf16[512,768]{1,0:T(8,128)(2,1)S(1)}, bf16[512,768]{1,0:T(8,128)(2,1)}, u32[]{:S(2)}) copy-start(bf16[512,768]{1,0:T(8,128)(2,1)} %convert_element_type.226) | copy-start | bytes 2359300
  404.1 315.9 %all-reduce.10.cloned.1.call-start = ((), (), s32[]{:S(2)}) async-start(), calls=%async_computation.19 | async-start | bytes 7077888 | tf_op jit(solution)/shard_map/psum | solution.py:267
  720.0 5.6 copy-start.33
  720.0 6.4 copy-start.22
  (58 other events, 148.0 us)
Sparse Core Ops, SparseCore 0:
  9.6 20.1 all-gather.12
  31.3 17.4 all-gather.10
  50.4 17.4 all-gather.8
  69.2 17.4 all-gather.14
  88.1 37.4 all-gather.16
  127.0 37.9 all-gather.18
  168.4 55.1 all-gather.20
  363.4 25.7 reduce-scatter.6
  392.3 25.6 reduce-scatter.8
  421.0 25.6 reduce-scatter.10
  449.2 25.6 reduce-scatter.12
  477.2 47.8 reduce-scatter.14
  527.6 47.9 reduce-scatter.16
  579.8 140.1 all-reduce.9

commit v2 on v1

--- a/solution.py
+++ b/solution.py
@@ -3,6 +3,8 @@
 import jax
 import jax.numpy as jnp
 from jax import lax
+from jax.experimental import pallas as pl
+from jax.experimental.pallas import tpu as pltpu
 from jax.sharding import PartitionSpec as P
 
 D = 768
@@ -101,6 +103,296 @@
     ).astype(jnp.bfloat16)
     output = middle + product(hidden_act, picture_perceptron_exit)
     return normalize(jnp.mean(output.reshape(examples, PATCHES, D), axis=1)).astype(jnp.bfloat16)
+
+
+MESH = pl.DeviceIdType.MESH
+ROWS = 128
+
+
+def bit_of(value, bit):
+    return lax.rem(lax.div(value, bit), 2)
+
+
+def peer(axis, bit):
+    dp, mp = lax.axis_index("dp"), lax.axis_index("mp")
+    if axis == "dp":
+        return (dp + bit - 2 * bit * bit_of(dp, bit), mp)
+    return (dp, mp + bit - 2 * bit * bit_of(mp, bit))
+
+
+def doubling_bits(dp_count):
+    bits, bit = [], 1
+    while bit < dp_count:
+        bits.append(("dp", bit))
+        bit *= 2
+    return bits
+
+
+def gradient_sum_kernel(dp_count, stack, small, out, small_out, keep, first, second, *rest):
+    dp_bits = doubling_bits(dp_count)
+    levels = len(dp_bits)
+    parts, (whole, small_in, small_sum, send, receive, load, store, small_send, small_receive) = (
+        rest[:levels],
+        rest[levels:],
+    )
+    bits = [("mp", 1), ("mp", 2)] + dp_bits
+    peers = [peer(*b) for b in bits]
+    low, high = bit_of(lax.axis_index("mp"), 1), bit_of(lax.axis_index("mp"), 2)
+    own = [bit_of(lax.axis_index("dp"), bit) for _, bit in dp_bits]
+    chunks = stack.shape[2] // ROWS
+    barrier = pltpu.get_barrier_semaphore()
+    for p in peers:
+        pl.semaphore_signal(barrier, inc=1, device_id=p, device_id_type=MESH)
+    pl.semaphore_wait(barrier, len(peers))
+
+    sizes = []
+    size = ROWS
+    for _ in dp_bits:
+        halve = size >= 32
+        size = size // 2 if halve else size
+        sizes.append((size, halve))
+
+    def add(target, other):
+        target[...] = (target[...].astype(jnp.float32) + other[...].astype(jnp.float32)).astype(
+            jnp.bfloat16
+        )
+
+    def rows(c):
+        return pl.ds(pl.multiple_of(c * ROWS, ROWS), ROWS)
+
+    def copy(stage, c):
+        if stage == 0:
+            source, target, who = stack.at[:, 1 - low, rows(c)], first.at[c], 0
+        elif stage == 1:
+            source, target, who = first.at[c, 1 - high], second.at[c], 1
+        elif stage < 2 + levels:
+            i = stage - 2
+            n, halve = sizes[i]
+            before = second if i == 0 else parts[i - 1]
+            source = before.at[c, pl.ds((1 - own[i]) * n, n)] if halve else before.at[c]
+            target, who = parts[i].at[c], stage
+        else:
+            i = gathers[stage - 2 - levels]
+            n = sizes[i][0]
+            where = sum(
+                own[j] * sizes[j][0] for j in range(i + 1) if sizes[j][1]
+            )
+            source = target = whole.at[c, pl.ds(where, n)]
+            who = 2 + i
+        return pltpu.make_async_remote_copy(
+            src_ref=source,
+            dst_ref=target,
+            send_sem=send.at[stage, c],
+            recv_sem=receive.at[stage, c],
+            device_id=peers[who],
+            device_id_type=MESH,
+        )
+
+    gathers = [i for i in reversed(range(levels)) if sizes[i][1]]
+    stages = 2 + levels + len(gathers)
+
+    def load_copy(c):
+        return pltpu.make_async_copy(stack.at[:, low, rows(c)], keep.at[c], load.at[c])
+
+    def store_copy(c):
+        return pltpu.make_async_copy(whole.at[c], out.at[rows(c)], store.at[c])
+
+    def finish(stage, c):
+        copy(stage, c).wait_recv()
+        if stage == 0:
+            load_copy(c).wait()
+            add(first.at[c], keep.at[c])
+        elif stage == 1:
+            add(second.at[c], first.at[c, high])
+        elif stage < 2 + levels:
+            i = stage - 2
+            n, halve = sizes[i]
+            before = second if i == 0 else parts[i - 1]
+            source = before.at[c, pl.ds(pl.multiple_of(own[i] * n, n), n)] if halve else before.at[c]
+            if i < levels - 1:
+                add(parts[i].at[c], source)
+            else:
+                where = sum(own[j] * sizes[j][0] for j in range(levels) if sizes[j][1])
+                whole.at[c, pl.ds(pl.multiple_of(where, n), n)][...] = (
+                    parts[i].at[c][...].astype(jnp.float32) + source[...].astype(jnp.float32)
+                ).astype(jnp.bfloat16)
+
+    def small_copy(i):
+        return pltpu.make_async_remote_copy(
+            src_ref=small if i == 0 else small_sum.at[i - 1],
+            dst_ref=small_in.at[i],
+            send_sem=small_send.at[i],
+            recv_sem=small_receive.at[i],
+            device_id=peers[i],
+            device_id_type=MESH,
+        )
+
+    small_copy(0).start()
+
+    @pl.loop(0, chunks + stages)
+    def _(t):
+        for slot in range(stages + 1):
+            c = t - slot
+
+            @pl.when((c >= 0) & (c < chunks))
+            def _():
+                if slot == 0:
+                    load_copy(c).start()
+                else:
+                    finish(slot - 1, c)
+                if slot < stages:
+                    copy(slot, c).start()
+                else:
+                    store_copy(c).start()
+
+        for i in range(len(bits)):
+
+            @pl.when(t == 2 * i + 1)
+            def _():
+                small_copy(i).wait_recv()
+                total = (small if i == 0 else small_sum.at[i - 1])[...] + small_in[i]
+                if i < len(bits) - 1:
+                    small_sum[i] = total
+                    small_copy(i + 1).start()
+                else:
+                    small_out[...] = total
+
+    for i in range(len(bits)):
+        small_copy(i).wait_send()
+
+    @pl.loop(0, chunks)
+    def _(c):
+        for stage in range(stages):
+            copy(stage, c).wait_send()
+        store_copy(c).wait()
+
+
+def gradient_sum(dp_count, stack, small):
+    levels = len(doubling_bits(dp_count))
+    chunks = stack.shape[2] // ROWS
+    sizes, size, halvings = [], ROWS, 0
+    for _ in range(levels):
+        halvings += size >= 32
+        size = size // 2 if size >= 32 else size
+        sizes.append(size)
+    stages = 2 + levels + halvings
+    half = jnp.bfloat16
+    return pl.pallas_call(
+        partial(gradient_sum_kernel, dp_count),
+        out_shape=(
+            jax.ShapeDtypeStruct(stack.shape[2:], half),
+            jax.ShapeDtypeStruct(small.shape, jnp.float32),
+        ),
+        in_specs=[pl.BlockSpec(memory_space=pl.ANY), pl.BlockSpec(memory_space=pltpu.VMEM)],
+        out_specs=(pl.BlockSpec(memory_space=pl.ANY), pl.BlockSpec(memory_space=pltpu.VMEM)),
+        scratch_shapes=[
+            pltpu.VMEM((chunks, 2, ROWS, D), half),
+            pltpu.VMEM((chunks, 2, ROWS, D), half),
+            pltpu.VMEM((chunks, ROWS, D), half),
+        ]
+        + [pltpu.VMEM((chunks, n, D), half) for n in sizes]
+        + [
+            pltpu.VMEM((chunks, ROWS, D), half),
+            pltpu.VMEM((levels + 2,) + small.shape, jnp.float32),
+            pltpu.VMEM((levels + 1,) + small.shape, jnp.float32),
+            pltpu.SemaphoreType.DMA((stages, chunks)),
+            pltpu.SemaphoreType.DMA((stages, chunks)),
+            pltpu.SemaphoreType.DMA((chunks,)),
+            pltpu.SemaphoreType.DMA((chunks,)),
+            pltpu.SemaphoreType.DMA((levels + 2,)),
+            pltpu.SemaphoreType.DMA((levels + 2,)),
+        ],
+        compiler_params=pltpu.CompilerParams(
+            collective_id=1, has_side_effects=True, vmem_limit_bytes=56 * 2**20
+        ),
+        name="gradient_sum",
+    )(stack, small)
+
+
+def column_sum_kernel(value, out, near, far, send, receive):
+    dp, mp = lax.axis_index("dp"), lax.axis_index("mp")
+    dp_count, mp_count = far.shape[0], near.shape[0]
+    barrier = pltpu.get_barrier_semaphore()
+    for step in range(1, mp_count):
+        pl.semaphore_signal(
+            barrier, inc=1, device_id=(dp, lax.rem(mp + step, mp_count)), device_id_type=MESH
+        )
+
+    @pl.loop(1, dp_count)
+    def _(step):
+        pl.semaphore_signal(
+            barrier, inc=1, device_id=(lax.rem(dp + step, dp_count), mp), device_id_type=MESH
+        )
+
+    pl.semaphore_wait(barrier, mp_count + dp_count - 2)
+
+    def near_copy(step, sender):
+        return pltpu.make_async_remote_copy(
+            src_ref=value,
+            dst_ref=near.at[sender],
+            send_sem=send.at[step],
+            recv_sem=receive.at[step],
+            device_id=(dp, lax.rem(mp + step, mp_count)),
+            device_id_type=MESH,
+        )
+
+    def far_copy(step, sender):
+        return pltpu.make_async_remote_copy(
+            src_ref=far.at[dp],
+            dst_ref=far.at[sender],
+            send_sem=send.at[mp_count + step],
+            recv_sem=receive.at[mp_count + step],
+            device_id=(lax.rem(dp + step, dp_count), mp),
+            device_id_type=MESH,
+        )
+
+    for step in range(1, mp_count):
+        near_copy(step, mp).start()
+    near[mp] = value[...]
+    for step in range(1, mp_count):
+        near_copy(step, lax.rem(mp + mp_count - step, mp_count)).wait_recv()
+    total = near[0]
+    for i in range(1, mp_count):
+        total = total + near[i]
+    far[dp] = total
+
+    @pl.loop(1, dp_count)
+    def _(step):
+        far_copy(step, dp).start()
+
+    @pl.loop(1, dp_count)
+    def _(step):
+        far_copy(step, lax.rem(dp + dp_count - step, dp_count)).wait_recv()
+
+    out[...] = far[0]
+
+    @pl.loop(1, dp_count)
+    def _(i):
+        out[...] += far[i]
+
+    for step in range(1, mp_count):
+        near_copy(step, mp).wait_send()
+
+    @pl.loop(1, dp_count)
+    def _(step):
+        far_copy(step, dp).wait_send()
+
+
+def column_sum(dp_count, mp_count, value):
+    return pl.pallas_call(
+        column_sum_kernel,
+        out_shape=jax.ShapeDtypeStruct(value.shape, jnp.float32),
+        in_specs=[pl.BlockSpec(memory_space=pltpu.VMEM)],
+        out_specs=pl.BlockSpec(memory_space=pltpu.VMEM),
+        scratch_shapes=[
+            pltpu.VMEM((mp_count,) + value.shape, jnp.float32),
+            pltpu.VMEM((dp_count,) + value.shape, jnp.float32),
+            pltpu.SemaphoreType.DMA((mp_count + dp_count,)),
+            pltpu.SemaphoreType.DMA((mp_count + dp_count,)),
+        ],
+        compiler_params=pltpu.CompilerParams(collective_id=2, has_side_effects=True),
+        name="column_sum",
+    )(value)
 
 
 def embed(block_out):
@@ -212,7 +504,9 @@
     row_weights = weights * image_mask[None, :]
     row_total = jnp.sum(row_weights, axis=1)
     column_weights = weights * own_text[:, None]
-    column_total = lax.psum(jnp.sum(column_weights, axis=0), ("dp", "mp"))
+    column_total = column_sum(
+        lax.axis_size("dp"), mp_count, jnp.sum(column_weights, axis=0).reshape(-1, 128)
+    ).reshape(-1)
     pair_total = jnp.sum(image_weight)
     safe_row = jnp.where(row_total > 0, row_total, 1.0)
     safe_column = jnp.where(column_total > 0, column_total, 1.0)
@@ -260,29 +554,49 @@
     norm_one_grads = norm_one_back(normed_one_grad)
     text_in_grad = middle_grad + norm_one_grads[0]
 
-    def share(grad, axis):
-        part = lax.psum_scatter(
-            grad.astype(jnp.bfloat16), "mp", scatter_dimension=axis, tiled=True
-        )
-        return lax.psum(part, "dp").astype(jnp.float32)
-
-    shared = lax.psum(
-        (
-            total_part,
-            temp_part,
-            norm_one_grads[1],
-            norm_one_grads[2],
-            attn_bias_grad,
-            norm_two_grads[1],
-            norm_two_grads[2],
-            proj_bias_grad,
-            query_bias_grad,
-            value_bias_grad,
-            hidden_bias_grad,
-        ),
-        ("dp", "mp"),
-    )
+    def quarters(grad):
+        return grad.astype(jnp.bfloat16).reshape(mp_count, -1, D)
+
+    scalars = jnp.stack([total_part, temp_part])
+    vectors = [
+        norm_one_grads[1],
+        norm_one_grads[2],
+        attn_bias_grad,
+        norm_two_grads[1],
+        norm_two_grads[2],
+        proj_bias_grad,
+        query_bias_grad,
+        value_bias_grad,
+        hidden_bias_grad,
+    ]
+    small = jnp.concatenate(vectors + [scalars])
+    filled = small.shape[0]
+    small = jnp.pad(small, (0, -filled % 1024)).reshape(-1, 128)
+    stack = jnp.concatenate(
+        [
+            quarters(w_proj_grad),
+            jnp.stack(jnp.split(w_hidden_grad.astype(jnp.bfloat16), mp_count, axis=1)),
+            quarters(w_query_grad.T),
+            quarters(w_key_grad.T),
+            quarters(w_value_grad.T),
+            quarters(w_attn_out_grad),
+        ],
+        axis=1,
+    )
+    own_grads, small = gradient_sum(
+        lax.axis_size("dp"), stack.reshape((2, 2) + stack.shape[1:]), small
+    )
+    small = small.reshape(-1)
+    shared, start = [], 0
+    for vector in vectors:
+        shared.append(small[start : start + vector.shape[0]])
+        start += vector.shape[0]
+    shared = [small[start], small[start + 1]] + shared
     loss = jnp.reshape((shared[0] + column_part) / pair_total, (1,))
+    quarter = D // mp_count
+
+    def rows_of(start, count):
+        return own_grads[start : start + count].astype(jnp.float32)
 
     def own(vector):
         return lax.dynamic_slice_in_dim(
@@ -296,18 +610,18 @@
         jnp.reshape(shared[1], (1,)),
         shared[2],
         shared[3],
-        share(w_query_grad, 1),
+        rows_of(2 * D, quarter).T,
         own(shared[8]),
-        share(w_key_grad, 1),
-        share(w_value_grad, 1),
+        rows_of(2 * D + 1 * quarter, quarter).T,
+        rows_of(2 * D + 2 * quarter, quarter).T,
         own(shared[9]),
-        share(w_attn_out_grad, 0),
+        rows_of(2 * D + 3 * quarter, quarter),
         shared[4],
         shared[5],
         shared[6],
-        share(w_hidden_grad, 1),
+        rows_of(D, D),
         own(shared[10]),
-        share(w_proj_grad, 0),
+        rows_of(0, D),
         shared[7],
     )
 

time: 745 us -> 521 us (0.70)
  waiting for transfers between devices: 258 us -> 3.72 us
  Pallas kernels: 0 us -> 121 us
  blocking collectives: 141 us -> 53.7 us
  matrix products: 160 us -> 147 us
  local copies, waits for them, and re-layouts: 110 us -> 121 us
    reduce_scatter x6 -> x0, waiting for transfers between devices: 171 us -> none  [share(): lax.psum_scatter(grad.astype(jnp.bfloat16), 'mp', scatter_dimension=axis,...]
    pallas_call x0 -> x2, Pallas kernels: none -> 121 us  [the longest x1 110 us: gradient_sum(): pl.pallas_call(partial(gradient_sum_kernel, dp_count), out_shape=(jax.Sha...]
    psum x2 -> x0, blocking collectives: 84.9 us -> none  [the longest x1 45.1 us: body(): lax.psum((total_part, temp_part, norm_one_grads[1], norm_one_grads[2], at...]
    psum x1 -> x0, waiting for transfers between devices: 83.1 us -> none  [share(): return lax.psum(part, 'dp').astype(jnp.float32)]
    unnamed x192 -> x189, local copies, waits for them, and re-layouts: 10.8 us -> 19.3 us
  transfers between devices with their start and end apart: 14 -> 7, of which waited for: 6 -> 0; matrix products, arithmetic and copies ran while one was open for 33% -> 39% of each run, Pallas kernels for 0% -> 0%
where the time goes in v2:
time: 521 us; the launch traced here: 513 us
  matrix products  147 us (28%)
  local copies, waits for them, and re-layouts  121 us (23%)
  Pallas kernels  121 us (23%)
  blocking collectives  53.7 us (10%)
  other arithmetic  44.8 us (9%)
  between operations  21.1 us (4%)
    pallas_call x1, Pallas kernels, gradient_sum(): pl.pallas_call(partial(gradient_sum_kernel, dp_count), out_shape=(jax.Sha...  110 us
    dot_general x13, matrix products, product(): return jnp.dot(left, right, preferred_element_type=jnp.float32)  71.2 us
    unnamed x2, blocking collectives  47.6 us
    convert_element_type x2, local copies, waits for them, and re-layouts, image_embed(): mixed_heads.reshape(examples * PATCHES, D).astype(jnp.bfloat16)  21.5 us
    unnamed x189, local copies, waits for them, and re-layouts  19.3 us
    dot_general x2, matrix products, masked_scores(): jnp.einsum('gqhd,gkhd->ghqk', queries, key_rows, preferred_element_type=j...  15.7 us
    sub x1, other arithmetic, softmax_rows(): weights = jnp.exp(scores - highest)  15.2 us
    pallas_call x1, Pallas kernels, column_sum(): pl.pallas_call(column_sum_kernel, out_shape=jax.ShapeDtypeStruct(value.sh...  11.8 us
  transfers between devices with their start and end apart: 7, of which 0 were waited for; matrix products, arithmetic and copies ran while one was open for 39% of the time, Pallas kernels for 0%

profile of v2, /device:TPU:0, one launch (start us, length us, event | category | flops | bytes accessed | tf_op | source)
XLA Modules:
  0.0 513.4 jit_solution(14531626418429301683)
XLA Ops:
  11.2 2.3 convert_reduce_fusion
  14.5 3.7 convolution_convert_fusion.3
  18.3 8.6 %reshape.317 = bf16[32,50,12,64]{3,2,1,0:T(8,128)(2,1)} reshape(bf16[1600,768]{1,0:T(8,128)(2,1)} %convolution_convert_fusion.3) | data formatting | bytes 4915200 | tf_op jit(solution)/shard_map/reshape | solution.py:84
  26.8 5.4 %convolution_convert_fusion.2 = bf16[1600,768]{1,0:T(8,128)(2,1)} fusion(bf16[768,768]{1,0:T(8,128)(2,1)S(1)} %copy-done.67, bf16[1600,768]{1,0:T(8,128)(2,1)} %param.31, f32[1600]{0:T(1024)S(1)} %add_rsqrt_fusion.1, f32[1600]{0:T(1024)S(1)} %broadcast_multiply_fusion.1), kind=kOutput, calls=%fused_computation.50 | convolution fusion | flops 1893580800 | bytes 6107648 | tf_op jit(solution)/shard_map/dot_general | solution.py:28
  32.2 8.6 %reshape.318 = bf16[32,50,12,64]{3,2,1,0:T(8,128)(2,1)} reshape(bf16[1600,768]{1,0:T(8,128)(2,1)} %convolution_convert_fusion.2) | data formatting | bytes 4915200 | tf_op jit(solution)/shard_map/reshape | solution.py:86
  40.8 12.2 %fusion.26 = f32[32,12,50,50]{2,3,1,0:T(8,128)} fusion(bf16[32,50,12,64]{3,2,1,0:T(8,128)(2,1)} %reshape.318, bf16[32,50,12,64]{3,2,1,0:T(8,128)(2,1)} %reshape.317), kind=kOutput, calls=%fused_computation.35 | convolution fusion | flops 122880000 | bytes 8755200 | tf_op jit(solution)/shard_map/gqhd,gkhd->ghqk/dot_general | solution.py:32
  53.0 15.2 %fusion.114 = (f32[32,12,50]{2,1,0:T(8,128)S(1)}, f32[32,12,50,50]{2,3,1,0:T(8,128)}) fusion(f32[32,12,50,50]{2,3,1,0:T(8,128)} %fusion.26), kind=kOutput, calls=%fused_computation.226 | output fusion | flops 3840049 | bytes 7756800 | tf_op jit(solution)/shard_map/sub | solution.py:43
  68.2 3.6 convolution_convert_fusion.4
  71.9 8.5 %reshape.316 = bf16[32,50,12,64]{3,2,1,0:T(8,128)(2,1)} reshape(bf16[1600,768]{1,0:T(8,128)(2,1)} %convolution_convert_fusion.4) | data formatting | bytes 4915200 | tf_op jit(solution)/shard_map/reshape | solution.py:89
  80.4 9.3 %convert_bitcast_fusion = bf16[32,50,12,64]{3,1,2,0:T(8,128)(2,1)} fusion(f32[32,12,50,50]{2,3,1,0:T(8,128)} %get-tuple-element.79, f32[32,12,50]{2,1,0:T(8,128)S(1)} %get-tuple-element.78, bf16[32,50,12,64]{3,2,1,0:T(8,128)(2,1)} %reshape.316), kind=kOutput, calls=%fused_computation.39 | convolution fusion | flops 126028800 | bytes 8832000 | tf_op jit(solution)/shard_map/ghqk,gkhd->gqhd/dot_general | solution.py:92
  89.7 9.7 %copy.116 = bf16[32,50,12,64]{1,0,3,2:T(8,128)(2,1)} copy(bf16[32,50,12,64]{3,1,2,0:T(8,128)(2,1)} %convert_bitcast_fusion) | data formatting | bytes 4915200 | tf_op jit(solution)/shard_map/convert_element_type | solution.py:98
  99.4 11.8 %convert_element_type.207 = bf16[1600,768]{0,1:T(8,128)(2,1)} reshape(bf16[32,50,12,64]{1,0,3,2:T(8,128)(2,1)} %copy.116) | data formatting | bytes 4915200 | tf_op jit(solution)/shard_map/convert_element_type | solution.py:98
  111.2 4.8 fusion.115
  118.2 23.4 %fusion.34 = f32[1600,768]{1,0:T(8,128)} fusion(f32[1600,768]{1,0:T(8,128)} %copy-done.16, bf16[3072,768]{1,0:T(8,128)(2,1)} %param.53, bf16[768,3072]{1,0:T(8,128)(2,1)} %param.52, f32[1600]{0:T(1024)S(1)} %add_rsqrt_fusion, f32[1600]{0:T(1024)S(1)} %broadcast_multiply_fusion), kind=kOutput, calls=%fused_computation.49 | convolution fusion | flops 15148646400 | bytes 19280384 | tf_op jit(solution)/shard_map/dot_general | solution.py:28
  141.6 5.6 %reshape.274 = f32[32,50,768]{2,1,0:T(8,128)} reshape(f32[1600,768]{1,0:T(8,128)} %fusion.34) | data formatting | bytes 9830400 | tf_op jit(solution)/shard_map/reshape | solution.py:105
  147.3 3.2 reduce_sum.395
  152.6 6.1 %all-gather = f32[4,1,768]{2,1,0:T(1,128)S(1)} all-gather(f32[1,1,768]{2,1,0:T(1,128)S(1)} %reshape.310), channel_id=1, replica_groups=mesh['dp'=8,'mp'=4] {'mp'}, dimensions={0}, use_global_device_ids=true | all-gather | bytes 15360 | tf_op jit(solution)/shard_map/all_gather | solution.py:447
  160.5 4.3 scatter_custom_fusion
  166.0 7.5 %all-reduce.6 = (f32[768]{0:T(1024)S(1)}, f32[768]{0:T(1024)S(1)}) all-reduce(f32[768]{0:T(1024)S(1)} %dynamic-update-slice.1, f32[768]{0:T(1024)S(1)} %dynamic-update-slice), channel_id=1, replica_groups=mesh['dp'=8,'mp'=4] {'mp'}, use_global_device_ids=true, to_apply=%add.2 | all-reduce | flops 1536 | bytes 12288
  173.7 40.1 %all-reduce.5 = (f32[1024]{0:T(1024)S(1)}, f32[1024]{0:T(1024)S(1)}) all-reduce(f32[1024]{0:T(1024)S(1)} %convert_dynamic-update-slice_fusion, f32[1024]{0:T(1024)S(1)} %convert_dynamic-update-slice_fusion.1), channel_id=1, replica_groups=mesh['dp'=8,'mp'=4] {'dp','mp'}, use_global_device_ids=true, to_apply=%add.3 | all-reduce | flops 2048 | bytes 16384
  213.8 8.8 %gather_fusion = f32[1024]{0:T(1024)} fusion(f32[1024]{0:T(1024)S(1)} %get-tuple-element.39, s32[1024]{0:T(1024)S(1)} %fusion.88), kind=kCustom, calls=%fused_computation | custom fusion | bytes 12288 | tf_op jit(solution)/shard_map/gather | solution.py:498
  222.7 2.2 add_convert_fusion.1
  224.9 2.2 reshape.268
  227.1 2.2 convolution_convert_fusion.12
  229.3 2.2 reshape.269
  231.6 2.2 add_convert_fusion.2
  233.8 2.2 reshape.267
  236.0 3.5 fusion.112
  244.2 4.1 convert_element_type.193
  248.3 2.7 fusion.113
  252.6 8.2 %fusion.99 = f32[512,3072]{1,0:T(8,128)} fusion(bf16[768,3072]{1,0:T(8,128)(2,1)} %all-gather.17.cloned.1.call-done, f32[512,768]{1,0:T(8,128)} %copy-done.13, f32[768]{0:T(1024)S(1)} %copy-done.74, f32[768]{0:T(1024)S(1)} %copy-done.57, f32[512]{0:T(512)S(1)} %fusion.92, f32[512]{0:T(512)S(1)} %broadcast_multiply_fusion.3), kind=kOutput, calls=%fused_computation.221 | convolution fusion | flops 2417885184 | bytes 12593152 | tf_op jit(solution)/shard_map/dot_general | solution.py:28
  260.8 9.6 %bitcast_reduce_fusion = (f32[32,768]{1,0:T(8,128)S(1)}, bf16[512,768]{1,0:T(8,128)(2,1)}) fusion(f32[768]{0:T(1024)S(1)} %copy-done.73, f32[512,768]{1,0:T(8,128)} %copy-done.13, bf16[3072,768]{1,0:T(8,128)(2,1)} %all-gather.19.cloned.1.call-done, f32[512,3072]{1,0:T(8,128)} %fusion.99, f32[3072]{0:T(1024)S(1)} %bitcast.126), kind=kOutput, calls=%fused_computation.88 | convolution fusion | flops 2433196032 | bytes 13483008 | tf_op jit(solution)/shard_map/dot_general | solution.py:28
  271.8 2.7 multiply_reduce_fusion.7
  274.5 11.8 %column_sum.1 = f32[8,128]{1,0:T(8,128)} custom-call(f32[8,128]{1,0:T(8,128)} %bitcast.125), custom_call_target="tpu_custom_call" | custom-call | tf_op jit(solution)/shard_map/column_sum/pallas_call | solution.py:382
  295.1 10.8 %convert_reduce_fusion.1 = (f32[3072]{0:T(1024)}, bf16[512,3072]{1,0:T(8,128)(2,1)S(1)}) fusion(f32[512,3072]{1,0:T(8,128)} %fusion.99, f32[3072]{0:T(1024)S(1)} %bitcast.127, bf16[512,768]{1,0:T(8,128)(2,1)S(1)} %bitcast_convert_fusion, bf16[3072,768]{1,0:T(8,128)(2,1)} %all-gather.19.cloned.1.call-done), kind=kOutput, calls=%fused_computation.30 | convolution fusion | flops 2452091904 | bytes 14966784 | tf_op jit(solution)/shard_map/rd,fd->rf/dot_general | solution.py:526
  306.0 3.5 multiply_reduce_fusion.3
  314.2 3.8 reshape.278
  318.0 2.8 convert_reduce_fusion.2
  326.1 2.2 convert_reduce_fusion.3
  328.5 4.9 convolution_convert_fusion
  333.4 5.7 %convolution_convert_fusion.1 = bf16[3072,768]{1,0:T(8,128)(2,1)} fusion(bf16[512,768]{1,0:T(8,128)(2,1)S(1)} %copy-done.31, f32[512,3072]{1,0:T(8,128)S(1)} %bitcast.132, f32[3072]{0:T(1024)S(1)} %bitcast.128), kind=kOutput, calls=%fused_computation.43 | convolution fusion | flops 2434007040 | bytes 11808768 | tf_op jit(solution)/shard_map/rf,rd->fd/dot_general | solution.py:525
  352.2 3.2 convolution_convert_fusion.10
  369.4 2.8 slice_bitcast_fusion.3
  373.1 2.4 constant_dynamic-update-slice_fusion.5
  376.1 2.5 constant_dynamic-update-slice_fusion.4
  383.6 109.6 %gradient_sum.1 = (bf16[2304,768]{1,0:T(8,128)(2,1)}, f32[80,128]{1,0:T(8,128)}) custom-call(bf16[2,2,2304,768]{3,2,1,0:T(8,128)(2,1)} %constant_dynamic-update-slice_fusion.stack, f32[80,128]{1,0:T(8,128)} %pad_bitcast_fusion.small), custom_call_target="tpu_custom_call" | custom-call | tf_op jit(solution)/shard_map/gradient_sum/pallas_call | solution.py:280
  493.2 4.3 slice_convert_fusion
  497.5 2.7 slice_convert_fusion.2
  (287 shorter events, 72.6 us)
Async XLA Ops:
  7.2 104.0 %copy-start = (bf16[768,768]{1,0:T(8,128)(2,1)S(1)}, bf16[768,768]{1,0:T(8,128)(2,1)}, u32[]{:S(2)}) copy-start(bf16[768,768]{1,0:T(8,128)(2,1)} %param.51) | copy-start | bytes 3538948
  7.2 215.5 %all-gather.11.cloned.1.call-start = ((), (), s32[]{:S(2)}) async-start(), calls=%async_computation.1 | async-start | bytes 1474560 | tf_op jit(solution)/shard_map/all_gather | solution.py:441
  7.9 219.2 %all-gather.13.cloned.1.call-start = ((), (), s32[]{:S(2)}) async-start(), calls=%async_computation.2 | async-start | bytes 1474560 | tf_op jit(solution)/shard_map/all_gather | solution.py:442
  8.7 222.9 %all-gather.9.cloned.1.call-start = ((), (), s32[]{:S(2)}) async-start(), calls=%async_computation | async-start | bytes 1474560 | tf_op jit(solution)/shard_map/all_gather | solution.py:443
  9.4 238.9 %all-gather.15.cloned.1.call-start = ((), (), s32[]{:S(2)}) async-start(), calls=%async_computation.3 | async-start | bytes 1474560 | tf_op jit(solution)/shard_map/all_gather | solution.py:444
  10.0 242.6 %all-gather.17.cloned.1.call-start = ((), (), s32[]{:S(2)}) async-start(), calls=%async_computation.4 | async-start | bytes 5898240 | tf_op jit(solution)/shard_map/all_gather | solution.py:446
  10.6 250.2 %all-gather.19.cloned.1.call-start = ((), (), s32[]{:S(2)}) async-start(), calls=%async_computation.5 | async-start | bytes 5898240 | tf_op jit(solution)/shard_map/all_gather | solution.py:446
  11.2 260.6 %all-gather.21.cloned.1.call-start = ((), (), s32[]{:S(2)}) async-start(), calls=%async_computation.6 | async-start | bytes 1622016 | tf_op jit(solution)/shard_map/all_gather | solution.py:459
  18.3 8.6 %copy-start.67 = (bf16[768,768]{1,0:T(8,128)(2,1)S(1)}, bf16[768,768]{1,0:T(8,128)(2,1)}, u32[]{:S(2)}) copy-start(bf16[768,768]{1,0:T(8,128)(2,1)} %param.49) | copy-start | bytes 3538948
  53.0 15.2 %copy-start.9 = (bf16[1600,768]{1,0:T(8,128)(2,1)S(1)}, bf16[1600,768]{1,0:T(8,128)(2,1)}, u32[]{:S(2)}) copy-start(bf16[1600,768]{1,0:T(8,128)(2,1)} %param.31) | copy-start | bytes 7372804
  53.0 15.2 %copy-start.68 = (bf16[768,768]{1,0:T(8,128)(2,1)S(1)}, bf16[768,768]{1,0:T(8,128)(2,1)}, u32[]{:S(2)}) copy-start(bf16[768,768]{1,0:T(8,128)(2,1)} %param.50) | copy-start | bytes 3538948
  147.2 4.2 copy-start.2
  147.2 4.8 copy-start.79
  147.3 5.3 %copy-start.55 = (f32[768]{0:T(1024)S(1)}, f32[768]{0:T(1024)}, u32[]{:S(2)}) copy-start(f32[768]{0:T(1024)} %param.45) | copy-start | bytes 9220
  147.3 11.4 %copy-start.56 = (s32[1024]{0:T(1024)S(1)}, s32[1024]{0:T(1024)}, u32[]{:S(2)}) copy-start(s32[1024]{0:T(1024)} %param.30) | copy-start | bytes 12292
  147.3 12.7 %copy-start.61 = (s32[32]{0:T(128)S(1)}, s32[32]{0:T(128)}, u32[]{:S(2)}) copy-start(s32[32]{0:T(128)} %param.28) | copy-start | bytes 388
  147.3 18.2 %copy-start.63 = (f32[192]{0:T(256)S(1)}, f32[192]{0:T(256)}, u32[]{:S(2)}) copy-start(f32[192]{0:T(256)} %param.39) | copy-start | bytes 2308
  147.3 18.5 %copy-start.64 = (f32[192]{0:T(256)S(1)}, f32[192]{0:T(256)}, u32[]{:S(2)}) copy-start(f32[192]{0:T(256)} %param.36) | copy-start | bytes 2308
  147.3 26.3 %copy-start.78 = (s32[32]{0:T(128)S(1)}, s32[32]{0:T(128)}, u32[]{:S(2)}) copy-start(s32[32]{0:T(128)} %param.29) | copy-start | bytes 388
  152.0 61.9 %copy-start.41 = (f32[512]{0:T(512)}, f32[512]{0:T(512)S(1)}, u32[]{:S(2)}) copy-start(f32[512]{0:T(512)S(1)} %fusion.54) | copy-start | bytes 6148
  158.7 102.1 %copy-start.45 = (f32[4,1,768]{2,1,0:T(1,128)}, f32[4,1,768]{2,1,0:T(1,128)S(1)}, u32[]{:S(2)}) copy-start(f32[4,1,768]{2,1,0:T(1,128)S(1)} %all-gather) | copy-start | bytes 36868
  213.8 8.9 %copy-start.38 = (f32[768]{0:T(1024)S(1)}, f32[768]{0:T(1024)}, u32[]{:S(2)}) copy-start(f32[768]{0:T(1024)} %param.33) | copy-start | bytes 9220
  213.8 8.9 %copy-start.76 = (f32[768]{0:T(1024)S(1)}, f32[768]{0:T(1024)}, u32[]{:S(2)}) copy-start(f32[768]{0:T(1024)} %param.34) | copy-start | bytes 9220
  248.3 4.1 copy-start.27
  248.3 4.1 copy-start.29
  251.0 9.8 %copy-start.39 = (f32[512]{0:T(512)}, f32[512]{0:T(512)S(1)}, u32[]{:S(2)}) copy-start(f32[512]{0:T(512)S(1)} %broadcast_multiply_fusion.3) | copy-start | bytes 6148
  252.4 8.4 %copy-start.43 = (f32[512]{0:T(512)}, f32[512]{0:T(512)S(1)}, u32[]{:S(2)}) copy-start(f32[512]{0:T(512)S(1)} %multiply_reduce_fusion.5) | copy-start | bytes 6148
  252.5 8.3 %copy-start.49 = (f32[512]{0:T(512)}, f32[512]{0:T(512)S(1)}, u32[]{:S(2)}) copy-start(f32[512]{0:T(512)S(1)} %fusion.92) | copy-start | bytes 6148
  252.5 8.3 %copy-start.73 = (f32[768]{0:T(1024)S(1)}, f32[768]{0:T(1024)}, u32[]{:S(2)}) copy-start(f32[768]{0:T(1024)} %param.47) | copy-start | bytes 9220
  286.3 5.6 %copy-start.4 = (bf16[1024,768]{1,0:T(8,128)(2,1)S(1)}, bf16[1024,768]{1,0:T(8,128)(2,1)}, u32[]{:S(2)}) copy-start(bf16[1024,768]{1,0:T(8,128)(2,1)} %all-gather.21.cloned.1.call-done) | copy-start | bytes 4718596
  286.3 7.7 %copy-start.20 = (f32[32,768]{1,0:T(8,128)S(1)}, f32[32,768]{1,0:T(8,128)}, u32[]{:S(2)}) copy-start(f32[32,768]{1,0:T(8,128)} %copy-done.19) | copy-start | bytes 294916
  290.0 5.0 copy-start.46
  294.1 11.9 %slice-start.2 = ((s8[4718592]{0:T(1024)(128)(4,1)}), s8[4194304]{0:T(1024)(128)(4,1)S(1)}, s32[]{:S(2)}) async-start(s8[4718592]{0:T(1024)(128)(4,1)} %bitcast.129), calls=%async_computation.9 | async-start | bytes 8388608
  295.0 10.9 %copy-start.30 = (bf16[512,768]{1,0:T(8,128)(2,1)}, bf16[512,768]{1,0:T(8,128)(2,1)S(1)}, u32[]{:S(2)}) copy-start(bf16[512,768]{1,0:T(8,128)(2,1)S(1)} %bitcast_convert_fusion) | copy-start | bytes 2359300
  295.0 10.9 %copy-start.14 = (f32[512,768]{1,0:T(8,128)S(1)}, f32[512,768]{1,0:T(8,128)}, u32[]{:S(2)}) copy-start(f32[512,768]{1,0:T(8,128)} %copy-done.13) | copy-start | bytes 4718596
  295.1 10.9 %copy-start.40 = (f32[512]{0:T(512)S(1)}, f32[512]{0:T(512)}, u32[]{:S(2)}) copy-start(f32[512]{0:T(512)} %copy-done.39) | copy-start | bytes 6148
  295.1 10.9 %copy-start.50 = (f32[512]{0:T(512)S(1)}, f32[512]{0:T(512)}, u32[]{:S(2)}) copy-start(f32[512]{0:T(512)} %copy-done.49) | copy-start | bytes 6148
  295.1 10.9 %copy-start.58 = (f32[768]{0:T(1024)S(1)}, f32[768]{0:T(1024)}, u32[]{:S(2)}) copy-start(f32[768]{0:T(1024)} %param.42) | copy-start | bytes 9220
  295.1 10.9 %slice-start.3 = ((s8[4718592]{0:T(1024)(128)(4,1)}), s8[524288]{0:T(1024)(128)(4,1)S(1)}, s32[]{:S(2)}) async-start(s8[4718592]{0:T(1024)(128)(4,1)} %bitcast.129), calls=%async_computation.10 | async-start | bytes 1048576
  323.9 4.5 copy-start.81
  326.1 7.3 %slice-start.4 = ((s8[6291456]{0:T(1024)(128)(4,1)}), s8[4194304]{0:T(1024)(128)(4,1)S(1)}, s32[]{:S(2)}) async-start(s8[6291456]{0:T(1024)(128)(4,1)} %bitcast.131), calls=%async_computation.11 | async-start | bytes 8388608
  328.5 4.9 copy-start.31
  328.5 4.9 copy-start.47
  328.5 4.9 slice-start.5
  333.4 5.7 %copy-start.32 = (bf16[512,768]{1,0:T(8,128)(2,1)S(1)}, bf16[512,768]{1,0:T(8,128)(2,1)}, u32[]{:S(2)}) copy-start(bf16[512,768]{1,0:T(8,128)(2,1)} %convert_element_type.193) | copy-start | bytes 2359300
  333.4 5.7 %copy-start.34 = (bf16[512,768]{1,0:T(8,128)(2,1)S(1)}, bf16[512,768]{1,0:T(8,128)(2,1)}, u32[]{:S(2)}) copy-start(bf16[512,768]{1,0:T(8,128)(2,1)} %copy-done.33) | copy-start | bytes 2359300
  364.7 7.5 %slice-start = ((s8[4718592]{0:T(1024)(128)(4,1)}), s8[524288]{0:T(1024)(128)(4,1)S(1)}, s32[]{:S(2)}) async-start(s8[4718592]{0:T(1024)(128)(4,1)} %bitcast.116), calls=%async_computation.7 | async-start | bytes 1048576
  493.2 12.0 %copy-start.1 = (bf16[768,768]{1,0:T(8,128)(2,1)S(1)}, bf16[768,768]{1,0:T(8,128)(2,1)}, u32[]{:S(2)}) copy-start(bf16[768,768]{1,0:T(8,128)(2,1)} %param.51) | copy-start | bytes 3538948
  (47 other events, 102.0 us)
Sparse Core Ops, SparseCore 0:
  9.6 20.1 all-gather.10
  31.3 17.4 all-gather.12
  50.4 17.4 all-gather.8
  69.2 17.4 all-gather.14
  88.1 37.4 all-gather.16
  127.0 37.4 all-gather.18
  168.0 55.1 all-gather.20
